TPU v7x, 256 devices: a whole 4x4x8 slice. The times are simulated.
256 devices in a mesh: vol: 64 (over z, y, core), dsg: 4 (over x).
Axes of the slice: x: 4, y: 4, z: 8, core: 2. Of those that a mesh axis runs over, the one named last changes fastest.
Arguments:
- fields: float32 [262144, 128], P('vol'), may hold values from -6 to 6
- far_geom: float32 [8, 131072], P(None, ('vol', 'dsg')), may hold values from -6 to 6, as said below
- far_block: int32 [131072, 1], P(('vol', 'dsg')), may hold values from 0 to 63; in each aligned block of 512 rows (0 to 511, 512 to 1023, ...) at most 20 rows name the same one
- far_cell: int32 [131072], P(('vol', 'dsg')), may hold values from 0 to 4095
- far_patch: int32 [131072], P(('vol', 'dsg')), may hold values from 0 to 95, as said below
- near_geom: float32 [8, 524288], P(None, ('vol', 'dsg')), may hold values from -6 to 6, as said below
- near_cell: int32 [524288], P(('vol', 'dsg')), may hold values from 0 to 4095
- near_patch: int32 [524288], P(('vol', 'dsg')), may hold values from 0 to 95, as said below
- adjacency: int32 [96, 4], replicated, may hold values from -1 to 95, as said below
Outputs:
- far_density: float32 [131072], P(('vol', 'dsg'))
- design_grad: float32 [96, 64, 64], P('dsg')
Inputs may be any that keep to these rules, and one draw needn't show every extreme that they name: `far_geom`: rows 0-2 and 6-7 lie in [0, 1). `near_geom`: rows 0-2 and 6-7 lie in [0, 1). `far_block`: the 512 far points of one device name each block at most 20 times. `far_patch`: the far and near points of one device lie on at most 4 design patches, the same set for both. `near_patch`: the far and near points of one device lie on at most 4 design patches, the same set for both. -1 marks a free side; where adjacency[k, s] = m >= 0, adjacency[m, s xor 1] = k.
All inputs are finite; a program needn't handle non-finite values.
Results may differ from a plain program's by a relative error of at most 0.0003.
Values sent between devices are 32-bit elements; how exact they have to be, the bound alone decides.
A program may use at most 128 MiB of HBM per device.

v0:
```python
import jax
import jax.numpy as jnp
import numpy as np
from jax import lax
from jax.sharding import PartitionSpec as P

CTRL = 64
PATCH_GRP = 4
SMOOTH_ITERS = 3


PENALTY = 4.0
SMOOTHING = 16.0
FLIPPED = np.array([1, 0, 3, 2], dtype=np.int32)


def bernstein(position):
    complement = 1.0 - position
    values = jnp.stack(
        [
            complement * complement * complement,
            3.0 * position * complement * complement,
            3.0 * position * position * complement,
            position * position * position,
        ]
    )
    slopes = jnp.stack(
        [
            -3.0 * complement * complement,
            3.0 * complement * complement - 6.0 * position * complement,
            6.0 * position * complement - 3.0 * position * position,
            3.0 * position * position,
        ]
    )
    return (values, slopes)


def tensor_basis(factor_x, factor_y, factor_z):
    product = factor_x[:, None, None, :] * factor_y[None, :, None, :] * factor_z[None, None, :, :]
    return product.reshape(-1, factor_x.shape[-1])


def evaluate(columns, coords):
    value_x, slope_x = bernstein(coords[0])
    value_y, slope_y = bernstein(coords[1])
    value_z, slope_z = bernstein(coords[2])
    basis_set = [
        tensor_basis(value_x, value_y, value_z),
        tensor_basis(slope_x, value_y, value_z),
        tensor_basis(value_x, slope_y, value_z),
        tensor_basis(value_x, value_y, slope_z),
    ]
    half_width = columns.shape[0] // 2
    state_part = columns[:half_width]
    adjoint_part = columns[half_width:]
    results = [jnp.sum(state_part * basis_kind, 0) for basis_kind in basis_set]
    results = results + [jnp.sum(adjoint_part * basis_kind, 0) for basis_kind in basis_set]
    return jnp.stack(results)


def density(values, normals):
    grad_state = values[1:4]
    grad_adjoint = values[5:8]
    normal_sq = jnp.sum(normals * normals, 0)
    inner_sum = jnp.sum(grad_state * grad_adjoint, 0)
    along_state = jnp.sum(grad_state * normals, 0)
    along_adjoint = jnp.sum(grad_adjoint * normals, 0)
    return (
        normal_sq * inner_sum
        - 2.0 * along_state * along_adjoint
        + PENALTY * normal_sq * values[0] * values[4]
    )


def spline_weights(param, span_count):
    scaled = param * span_count
    first_span = jnp.clip(jnp.floor(scaled), 0, span_count - 1)
    offset_in = scaled - first_span
    complement = 1.0 - offset_in
    cubed = offset_in * offset_in * offset_in
    squared = offset_in * offset_in
    weights = jnp.stack(
        [
            complement * complement * complement / 6.0,
            (3.0 * cubed - 6.0 * squared + 4.0) / 6.0,
            (-3.0 * cubed + 3.0 * squared + 3.0 * offset_in + 1.0) / 6.0,
            cubed / 6.0,
        ]
    )
    return (first_span.astype(jnp.int32), weights)


def spline_matrix(param, control):
    start, weights = spline_weights(param, control - 3)
    columns = jnp.arange(control, dtype=jnp.int32)
    matrix = jnp.zeros((param.shape[0], control), jnp.float32)
    for offset in range(4):
        matrix = matrix + jnp.where(
            (start + offset)[:, None] == columns[None, :], weights[offset][:, None], 0.0
        )
    return matrix


def local_grid(strength, spline_params, patch_ids, slot_ids, slot_live, control):
    weights_s = spline_matrix(spline_params[0], control)
    weights_t = spline_matrix(spline_params[1], control)
    selector = ((patch_ids[:, None] == slot_ids[None, :]) & slot_live[None, :]).astype(jnp.float32)
    left = ((selector * strength[:, None])[:, :, None] * weights_s[:, None, :]).reshape(
        strength.shape[0], -1
    )
    result = jnp.einsum(
        "na,nb->ab",
        left,
        weights_t,
        precision=lax.Precision.HIGHEST,
        preferred_element_type=jnp.float32,
    )
    return result.reshape(slot_ids.shape[0], control, control)


def edge_table(iterate):
    return jnp.stack([iterate[:, 0, :], iterate[:, -1, :], iterate[:, :, 0], iterate[:, :, -1]], 1)


def lookup(edge_rows, neighbours):
    total_rows = edge_rows.shape[0] * 4
    wanted = (neighbours * 4 + FLIPPED[None, :]).reshape(-1)
    present = (neighbours >= 0).reshape(-1)
    selector = (
        (wanted[:, None] == jnp.arange(total_rows, dtype=jnp.int32)[None, :]) & present[:, None]
    ).astype(jnp.float32)
    picked = jnp.dot(
        selector,
        edge_rows.reshape(total_rows, -1),
        precision=lax.Precision.HIGHEST,
        preferred_element_type=jnp.float32,
    )
    return picked.reshape(neighbours.shape[0], 4, -1)


def apply_operator(iterate, halo_rows):
    patch_count, edge_size = (iterate.shape[0], iterate.shape[1])
    padded = jnp.zeros((patch_count, edge_size + 2, edge_size + 2), iterate.dtype)
    padded = padded.at[:, 1:-1, 1:-1].set(iterate)
    padded = padded.at[:, 0, 1:-1].set(halo_rows[:, 0])
    padded = padded.at[:, -1, 1:-1].set(halo_rows[:, 1])
    padded = padded.at[:, 1:-1, 0].set(halo_rows[:, 2])
    padded = padded.at[:, 1:-1, -1].set(halo_rows[:, 3])
    beside = padded[:, :-2, 1:-1] + padded[:, 2:, 1:-1] + padded[:, 1:-1, :-2] + padded[:, 1:-1, 2:]
    return iterate + SMOOTHING * (4.0 * iterate - beside)


def precondition(residual):
    patch_count, edge_size = (residual.shape[0], residual.shape[1])
    below_diag = jnp.full((patch_count, edge_size), -SMOOTHING, residual.dtype).at[:, 0].set(0.0)
    main_diag = jnp.full((patch_count, edge_size), 1.0 + 2.0 * SMOOTHING, residual.dtype)
    above_diag = jnp.full((patch_count, edge_size), -SMOOTHING, residual.dtype).at[:, -1].set(0.0)
    along_rows = lax.linalg.tridiagonal_solve(below_diag, main_diag, above_diag, residual)
    along_cols = lax.linalg.tridiagonal_solve(
        below_diag, main_diag, above_diag, jnp.swapaxes(along_rows, 1, 2)
    )
    return jnp.swapaxes(along_cols, 1, 2)


def keep_table(edge_rows):
    return edge_rows


def smooth(summed, neighbours, edges_of):
    iterate = precondition(summed)
    for sweep_index in range(SMOOTH_ITERS):
        halo_rows = lookup(edges_of(edge_table(iterate)), neighbours)
        iterate = iterate + precondition(summed - apply_operator(iterate, halo_rows))
    return iterate


def per_device(
    fields, far_geom, far_block, far_cell, far_patch, near_geom, near_cell, near_patch, adjacency
):
    vol_count = lax.axis_size("vol")
    far_count = far_cell.shape[0]
    capacity = 5 * far_count // (2 * vol_count)
    patches = adjacency.shape[0]
    control = CTRL
    group = PATCH_GRP
    patch_range = jnp.arange(patches, dtype=jnp.int32)
    present = jnp.any(near_patch[:, None] == patch_range[None, :], 0)
    present = present | jnp.any(far_patch[:, None] == patch_range[None, :], 0)
    rank = jnp.cumsum(present.astype(jnp.int32)) - 1
    matches = present[None, :] & (rank[None, :] == jnp.arange(group, dtype=jnp.int32)[:, None])
    slot_ids = jnp.sum(matches.astype(jnp.int32) * patch_range[None, :], 1)
    slot_live = jnp.any(matches, 1)
    near_count = near_cell.shape[0]
    block_len = min(4096, near_count)
    blocks = near_count // block_len

    def near_block(carried, inputs):
        geom_part, cells_part, patch_part = inputs
        rows = jnp.take(fields, cells_part, axis=0).T
        strength = density(evaluate(rows, geom_part[0:3]), geom_part[3:6])
        return (
            carried
            + local_grid(strength, geom_part[6:8], patch_part, slot_ids, slot_live, control),
            None,
        )

    start_grid = jnp.zeros((group, control, control), jnp.float32)
    grid_local, unused = lax.scan(
        near_block,
        start_grid,
        (
            near_geom.reshape(8, blocks, block_len).transpose(1, 0, 2),
            near_cell.reshape(blocks, block_len),
            near_patch.reshape(blocks, block_len),
        ),
    )
    target = far_block[:, 0]
    onehot_dest = (target[:, None] == jnp.arange(vol_count, dtype=jnp.int32)[None, :]).astype(
        jnp.int32
    )
    before = jnp.cumsum(onehot_dest, 0) - onehot_dest
    slot_rank = jnp.sum(before * onehot_dest, 1)
    slot_of = target * capacity + slot_rank
    request = jnp.zeros((1, vol_count * capacity), jnp.int32).at[0, slot_of].set(far_cell)
    request = request.reshape(1, vol_count, capacity)
    incoming = lax.all_to_all(request, "vol", split_axis=1, concat_axis=1, tiled=True)
    picked = jnp.take(fields, incoming.reshape(-1), axis=0).T
    picked = picked.reshape(fields.shape[1], incoming.shape[1], incoming.shape[2])
    replies = lax.all_to_all(picked, "vol", split_axis=1, concat_axis=1, tiled=True)
    placed = jnp.zeros((3, vol_count * capacity), jnp.float32).at[:, slot_of].set(far_geom[0:3])
    slot_values = evaluate(replies.reshape(replies.shape[0], -1), placed)
    far_values = jnp.take(slot_values, slot_of, axis=1)
    far_strength = density(far_values, far_geom[3:6])
    grid_local = grid_local + local_grid(
        far_strength, far_geom[6:8], far_patch, slot_ids, slot_live, control
    )
    placing = ((patch_range[:, None] == slot_ids[None, :]) & slot_live[None, :]).astype(jnp.float32)
    owner_count = lax.axis_size("dsg")
    per_owner = patches // owner_count
    owner_index = lax.axis_index("dsg")
    grid_whole = jnp.dot(
        placing,
        grid_local.reshape(group, -1),
        precision=lax.Precision.HIGHEST,
        preferred_element_type=jnp.float32,
    )
    summed = lax.psum(grid_whole, ("vol", "dsg")).reshape(patches, control, control)
    design = smooth(summed, adjacency, keep_table)
    design = lax.dynamic_slice_in_dim(design, owner_index * per_owner, per_owner, 0)
    return (far_strength, design)


def solution(mesh):
    return jax.shard_map(
        per_device,
        mesh=mesh,
        in_specs=(
            P("vol", None),
            P(None, ("vol", "dsg")),
            P(("vol", "dsg"), None),
            P(("vol", "dsg")),
            P(("vol", "dsg")),
            P(None, ("vol", "dsg")),
            P(("vol", "dsg")),
            P(("vol", "dsg")),
            P(),
        ),
        out_specs=(P(("vol", "dsg")), P("dsg", None, None)),
        check_vma=False,
    )
```

profile of v0, /device:TPU:1, one launch (start us, length us, event | category | flops | bytes accessed | tf_op | source)
XLA Modules:
  0.0 597.8 jit_solution(6945396377052510805)
XLA Ops:
  11.5 2.6 scatter_custom_fusion
  14.9 13.2 %all-to-all-start = ((s32[1,64,20]{2,0,1:T(1,128)}), s32[1,64,20]{2,0,1:T(1,128)S(1)}, u32[]{:S(2)}, u32[]{:S(2)}) async-start(s32[1,64,20]{2,0,1:T(1,128)} %bitcast.5), calls=%async_computation | async-start | bytes 65536 | tf_op jit(solution)/shard_map/all_to_all | solution.py:226
  28.0 1.7 slice_multiply_fusion.4
  42.7 1.9 scatter_custom_fusion.1
  56.8 2.0 mul.70953
  58.8 2.4 copy.7291
  61.2 2.0 mul.70965
  63.2 2.4 copy.7292
  65.6 2.0 mul.70978
  67.6 2.4 copy.7296
  70.0 4.6 mul.70848
  74.6 3.5 copy.7280
  78.1 4.4 mul.70860
  82.6 3.6 copy.7281
  86.2 4.4 mul.70872
  90.6 3.6 copy.7282
  94.2 3.8 mul.70882
  97.9 3.5 copy.7283
  101.8 7.6 %gather_fusion.2 = f32[2048,128]{1,0:T(8,128)} fusion(f32[4096,128]{1,0:T(8,128)S(1)} %copy-done, s32[2048]{0:T(1024)S(1)} %get-tuple-element.1882), kind=kCustom, calls=%fused_computation.2 | custom fusion | bytes 2105344 | tf_op jit(solution)/shard_map/while/body/eval_jaxpr/jit(_take)/gather | solution.py:199
  109.4 3.1 gather_fusion
  116.2 10.4 %all-to-all-start.1 = ((f32[128,64,20]{0,2,1:T(8,128)}), f32[128,64,20]{0,2,1:T(8,128)S(1)}, u32[]{:S(2)}, u32[]{:S(2)}) async-start(f32[128,64,20]{0,2,1:T(8,128)} %reshape.315135), calls=%async_computation.1 | async-start | bytes 1572864 | tf_op jit(solution)/shard_map/all_to_all | solution.py:229
  129.0 2.6 multiply_reduce_fusion.7
  131.8 17.6 %all-to-all-done.1 = f32[128,64,20]{0,2,1:T(8,128)S(1)} async-done(((f32[128,64,20]{0,2,1:T(8,128)}), f32[128,64,20]{0,2,1:T(8,128)S(1)}, u32[]{:S(2)}, u32[]{:S(2)}) %all-to-all-start.1) | async-done | bytes 655392 | tf_op jit(solution)/shard_map/all_to_all | solution.py:229
  149.4 3.8 multiply_reduce_fusion.8
  157.5 2.0 fusion.16
  159.6 3.1 fusion.83
  163.5 256.3 %all-reduce.6.cloned.1.call-done = f32[96,64,64]{0,2,1:T(8,128)} async-done(((f32[96,64,64]{0,2,1:T(8,128)}), f32[96,64,64]{0,2,1:T(8,128)}) %all-reduce.6.cloned.1.call-update) | async-done | bytes 1572880 | tf_op jit(solution)/shard_map/psum | solution.py:247
  419.8 1.7 slice_bitcast_fusion.7
  436.7 4.8 multiply_subtract_fusion.370
  441.6 9.9 %concatenate.199 = f32[63,96,64]{1,0,2:T(8,128)S(1)} concatenate(f32[1,96,64]{1,0,2:T(1,128)} %get-tuple-element.1225, f32[1,96,64]{1,0,2:T(1,128)} %get-tuple-element.1226, f32[1,96,64]{1,0,2:T(1,128)} %get-tuple-element.1227, f32[1,96,64]{1,0,2:T(1,128)} %get-tuple-element.1228, f32[1,96,64]{1,0,2:T(1,128)} %get-tuple-element.1229, f32[1,96,64]{1,0,2:T(1,128)} %get-tuple-element.1230, ...), dimensions={0} | concatenate | bytes 3096576 | tf_op jit(solution)/shard_map/vmap()/concatenate | solution.py:158
  457.8 2.2 scatter.69
  463.0 3.3 fusion.11
  468.7 2.7 multiply_subtract_fusion.308
  475.8 2.7 broadcast_multiply_fusion.14
  489.2 2.2 scatter.76
  494.2 3.0 fusion.7
  505.7 1.7 subtract_multiply_fusion.142
  514.4 4.7 multiply_subtract_fusion.124
  519.1 15.6 %concatenate.207 = f32[63,96,64]{1,0,2:T(8,128)} concatenate(f32[1,96,64]{1,0,2:T(1,128)S(1)} %get-tuple-element.820, f32[1,96,64]{1,0,2:T(1,128)S(1)} %get-tuple-element.821, f32[1,96,64]{1,0,2:T(1,128)S(1)} %get-tuple-element.822, f32[1,96,64]{1,0,2:T(1,128)} %get-tuple-element.823, f32[1,96,64]{1,0,2:T(1,128)} %get-tuple-element.824, f32[1,96,64]{1,0,2:T(1,128)} %get-tuple-element.825, ...), dimensions={0} | concatenate | bytes 3096576 | tf_op jit(solution)/shard_map/vmap()/concatenate | solution.py:158
  534.6 2.0 fusion.12
  542.9 2.2 scatter.85
  545.7 3.0 fusion.3
  549.9 1.8 subtract_multiply_fusion.100
  551.8 4.3 multiply_subtract_fusion.62
  568.7 4.9 multiply_subtract_fusion
  573.6 9.8 %concatenate.211 = f32[63,96,64]{1,0,2:T(8,128)S(1)} concatenate(f32[1,96,64]{1,0,2:T(1,128)S(1)} %get-tuple-element.656, f32[1,96,64]{1,0,2:T(1,128)S(1)} %get-tuple-element.657, f32[1,96,64]{1,0,2:T(1,128)S(1)} %get-tuple-element.658, f32[1,96,64]{1,0,2:T(1,128)} %get-tuple-element.659, f32[1,96,64]{1,0,2:T(1,128)} %get-tuple-element.660, f32[1,96,64]{1,0,2:T(1,128)} %get-tuple-element.661, ...), dimensions={0} | concatenate | bytes 3096576 | tf_op jit(solution)/shard_map/vmap()/concatenate | solution.py:158
  585.1 2.5 dynamic-slice_add_fusion
  587.5 3.2 copy.8826
  (878 shorter events, 118.6 us)
Async XLA Ops:
  7.2 94.6 %copy-start = (f32[4096,128]{1,0:T(8,128)S(1)}, f32[4096,128]{1,0:T(8,128)}, u32[]{:S(2)}) copy-start(f32[4096,128]{1,0:T(8,128)} %param.58) | copy-start | bytes 6291460
  11.5 31.2 %copy-start.118 = (s32[512,1]{0,1:T(1,128)}, s32[512,1]{0,1:T(1,128)S(1)}, u32[]{:S(2)}) copy-start(s32[512,1]{0,1:T(1,128)S(1)} %get-tuple-element.1367) | copy-start | bytes 6148
  14.9 86.7 %all-to-all-start = ((s32[1,64,20]{2,0,1:T(1,128)}), s32[1,64,20]{2,0,1:T(1,128)S(1)}, u32[]{:S(2)}, u32[]{:S(2)}) async-start(s32[1,64,20]{2,0,1:T(1,128)} %bitcast.5), calls=%async_computation | async-start | bytes 65536 | tf_op jit(solution)/shard_map/all_to_all | solution.py:226
  49.9 3.5 copy-start.88
  49.9 3.5 copy-start.89
  50.0 4.5 copy-start.119
  94.2 7.3 %copy-start.102 = (f32[3,512]{1,0:T(4,128)S(1)}, f32[3,512]{1,0:T(4,128)}, u32[]{:S(2)}) copy-start(f32[3,512]{1,0:T(4,128)} %get-tuple-element.1815) | copy-start | bytes 18436
  97.9 3.8 copy-start.101
  113.9 13.2 %copy-start.109 = (pred[2048]{0:T(1024)(128)(4,1)S(1)}, pred[2048]{0:T(1024)(128)(4,1)}, u32[]{:S(2)}) copy-start(pred[2048]{0:T(1024)(128)(4,1)} %compare_and_fusion) | copy-start | bytes 6148
  116.2 12.6 %copy-start.8 = (f32[64,2048]{0,1:T(8,128)S(1)}, f32[64,2048]{0,1:T(8,128)}, u32[]{:S(2)}) copy-start(f32[64,2048]{0,1:T(8,128)} %copy.7291) | copy-start | bytes 1572868
  116.2 33.2 %all-to-all-start.1 = ((f32[128,64,20]{0,2,1:T(8,128)}), f32[128,64,20]{0,2,1:T(8,128)S(1)}, u32[]{:S(2)}, u32[]{:S(2)}) async-start(f32[128,64,20]{0,2,1:T(8,128)} %reshape.315135), calls=%async_computation.1 | async-start | bytes 1572864 | tf_op jit(solution)/shard_map/all_to_all | solution.py:229
  126.6 293.1 %all-reduce.6.cloned.1.call-start = ((), (), s32[]{:S(2)}) async-start(), calls=%async_computation.2 | async-start | bytes 4194304 | tf_op jit(solution)/shard_map/psum | solution.py:247
  131.8 23.8 %copy-start.133 = (pred[512]{0:T(512)(128)(4,1)S(1)}, pred[512]{0:T(512)(128)(4,1)}, u32[]{:S(2)}) copy-start(pred[512]{0:T(512)(128)(4,1)} %get-tuple-element.1366) | copy-start | bytes 1540
  153.2 3.4 copy-start.121
  153.2 3.5 copy-start.87
  153.2 3.5 copy-start.134
  153.2 3.5 copy-start.135
  153.2 3.5 copy-start.136
  153.2 3.5 copy-start.137
  153.2 3.5 copy-start.138
  153.2 3.5 copy-start.139
  153.2 3.5 copy-start.140
  153.2 3.5 copy-start.141
  153.3 4.1 copy-start.79
  153.3 4.1 copy-start.123
  153.3 4.1 copy-start.124
  153.3 4.1 copy-start.125
  153.3 4.1 copy-start.126
  153.3 4.1 copy-start.127
  153.3 4.1 copy-start.128
  153.3 4.1 copy-start.129
  153.3 4.1 copy-start.130
  156.6 6.2 %copy-start.122 = (f32[512]{0:T(512)}, f32[512]{0:T(512)S(1)}, u32[]{:S(2)}) copy-start(f32[512]{0:T(512)S(1)} %multiply_add_fusion.2) | copy-start | bytes 6148
  159.6 3.8 copy-start.120
  159.6 3.8 copy-start.142
  430.5 11.1 %copy-start.80 = (f32[96,64]{0,1:T(8,128)}, f32[96,64]{0,1:T(8,128)S(1)}, u32[]{:S(2)}) copy-start(f32[96,64]{0,1:T(8,128)S(1)} %get-tuple-element.1210) | copy-start | bytes 73732
  430.5 11.1 %copy-start.83 = (f32[96,64]{0,1:T(8,128)}, f32[96,64]{0,1:T(8,128)S(1)}, u32[]{:S(2)}) copy-start(f32[96,64]{0,1:T(8,128)S(1)} %get-tuple-element.1211) | copy-start | bytes 73732
  430.5 21.0 %copy-start.75 = (f32[96,64]{0,1:T(8,128)}, f32[96,64]{0,1:T(8,128)S(1)}, u32[]{:S(2)}) copy-start(f32[96,64]{0,1:T(8,128)S(1)} %get-tuple-element.1202) | copy-start | bytes 73732
  436.6 5.0 copy-start.11
  436.6 4.9 copy-start.15
  436.6 4.9 copy-start.19
  436.7 4.9 copy-start.23
  436.7 4.9 copy-start.27
  436.7 4.9 copy-start.31
  519.0 15.6 %copy-start.5 = (f32[96,64,64]{0,2,1:T(8,128)S(1)}, f32[96,64,64]{0,2,1:T(8,128)}, u32[]{:S(2)}) copy-start(f32[96,64,64]{0,2,1:T(8,128)} %copy-done.4) | copy-start | bytes 4718596
  519.0 15.6 %copy-start.86 = (f32[96,64]{0,1:T(8,128)S(1)}, f32[96,64]{0,1:T(8,128)}, u32[]{:S(2)}) copy-start(f32[96,64]{0,1:T(8,128)} %get-tuple-element.800) | copy-start | bytes 73732
  573.6 9.8 %copy-start.85 = (f32[96,64]{0,1:T(8,128)S(1)}, f32[96,64]{0,1:T(8,128)}, u32[]{:S(2)}) copy-start(f32[96,64]{0,1:T(8,128)} %get-tuple-element.636) | copy-start | bytes 73732
  585.1 5.6 copy-start.1
  (98 other events, 177.4 us)
Sparse Core Ops, SparseCore 0:
  162.9 256.8 all-reduce.5
where the time goes:
time: 609 us; the launch traced here: 598 us
  waiting for transfers between devices  274 us (45%)
  local copies, waits for them, and re-layouts  155 us (25%)
  other arithmetic  114 us (19%)
  starting transfers between devices  24 us (4%)
  between operations  20.4 us (3%)
  matrix products  10.6 us (2%)
    psum x1, waiting for transfers between devices, per_device(): lax.psum(grid_whole, ('vol', 'dsg')).reshape(patches, control, control)  256 us
    mul x16, local copies, waits for them, and re-layouts, tensor_basis(): factor_x[:, None, None, :] * factor_y[None, :, None, :]  47 us
    sub x37, other arithmetic, precondition(): lax.linalg.tridiagonal_solve(below_diag, main_diag, above_diag, residual)  42 us
    concatenate x3, local copies, waits for them, and re-layouts, precondition(): lax.linalg.tridiagonal_solve(below_diag, main_diag, above_diag, residual)  35.3 us
    all_to_all x1, waiting for transfers between devices, per_device(): lax.all_to_all(picked, 'vol', split_axis=1, concat_axis=1, tiled=True)  17.6 us
    unnamed x515, local copies, waits for them, and re-layouts  16 us
    all_to_all x1, starting transfers between devices, per_device(): lax.all_to_all(request, 'vol', split_axis=1, concat_axis=1, tiled=True)  13.2 us
  transfers between devices with their start and end apart: 3, of which 2 were waited for; matrix products, arithmetic and copies ran while one was open for 13% of the time, Pallas kernels for 0%

commit v1 on v0

v1 whole, which is shorter than its diff:
```python
import jax
import jax.numpy as jnp
import numpy as np
from jax import lax
from jax.experimental import pallas as pl
from jax.experimental.pallas import tpu as pltpu
from jax.sharding import PartitionSpec as P

F32 = jnp.float32
BF16 = jnp.bfloat16
I32 = jnp.int32
MESH = pl.DeviceIdType.MESH

CTRL = 64
GROUP = 4
CAP = 20
PENALTY = 4.0
SMOOTHING = 16.0
LANES = 128
VOL = 64
DSG = 4
PATCHES = 96
OWN = PATCHES // DSG
HALF = OWN // 2
ROW = OWN * CTRL
NOBODY = 999.0


def constants():
    order = np.arange(1, CTRL + 1)
    sine = np.sqrt(2.0 / (CTRL + 1)) * np.sin(np.pi * np.outer(order, order) / (CTRL + 1))
    spectrum = 2.0 - 2.0 * np.cos(np.pi * order / (CTRL + 1))
    inverse = 1.0 / (1.0 + SMOOTHING * spectrum)
    power = [inverse * (1.0 - inverse) ** k for k in range(4)]
    ends = [sine[0], sine[-1]]
    zero = np.zeros((CTRL, CTRL))
    sine_pair = np.block([[sine, zero], [zero, sine]])
    total = sum(np.outer(p, p) for p in power)
    total_pair = np.concatenate([total, total], 1)

    def spread(k):
        scale = SMOOTHING * np.outer(power[k], power[k])
        table = np.zeros((4, CTRL, 4, CTRL))
        for side in range(4):
            for at in range(CTRL):
                unit = np.zeros(CTRL)
                unit[at] = 1.0
                end = ends[side % 2]
                field = scale * (np.outer(end, unit) if side < 2 else np.outer(unit, end))
                table[side, at, 0] = ends[0] @ field
                table[side, at, 1] = ends[1] @ field
                table[side, at, 2] = field @ ends[0]
                table[side, at, 3] = field @ ends[1]
        return table.reshape(4 * CTRL, 4 * CTRL)

    first = np.zeros((8, CTRL))
    lane_power = np.zeros((8, LANES))
    pair_first = np.zeros((16, LANES))
    pair_power = np.zeros((16, CTRL))
    for k in range(3):
        for side in range(2):
            row = 2 * k + side
            first[row] = power[k] * ends[side]
            lane_power[row] = np.tile(power[k], 2)
            for half in range(2):
                pair_first[6 * half + row, half * CTRL:(half + 1) * CTRL] = power[k] * ends[side]
                pair_power[6 * half + row] = power[k]
    tables = (sine, sine_pair, total_pair, spread(0), spread(1), first, lane_power, pair_first, pair_power)
    return [np.asarray(t, np.float32) for t in tables]


def iota(shape, axis):
    return lax.broadcasted_iota(I32, shape, axis)


def mm(a, b):
    return jnp.dot(a, b, preferred_element_type=F32)


def mm_nt(a, b):
    return lax.dot_general(a, b, (((1,), (1,)), ((), ())), preferred_element_type=F32)


def mm_tn(a, b):
    return lax.dot_general(a, b, (((0,), (0,)), ((), ())), preferred_element_type=F32)


def split2(x):
    high = x.astype(BF16)
    return high, (x - high.astype(F32)).astype(BF16)


def split3(x):
    high = x.astype(BF16)
    rest = x - high.astype(F32)
    middle = rest.astype(BF16)
    return high, middle, (rest - middle.astype(F32)).astype(BF16)


def exact(product, picks, x):
    high, middle, low = split3(x)
    picks = picks.astype(BF16)
    return product(picks, high) + product(picks, middle) + product(picks, low)


def dot3(product, a, b):
    a_high, a_low = split2(a)
    b_high, b_low = split2(b)
    return product(a_high, b_high) + product(a_high, b_low) + product(a_low, b_high)


def bernstein(t):
    c = 1.0 - t
    values = [c * c * c, 3.0 * t * c * c, 3.0 * t * t * c, t * t * t]
    slopes = [-3.0 * c * c, 3.0 * c * c - 6.0 * t * c, 6.0 * t * c - 3.0 * t * t, 3.0 * t * t]
    return values, slopes


def pick(index, rows):
    return jnp.where(
        index == 0, rows[0], jnp.where(index == 1, rows[1], jnp.where(index == 2, rows[2], rows[3]))
    )


def densities(columns, coords, normals):
    count = columns.shape[1]
    value_x, slope_x = bernstein(coords[0])
    value_y, slope_y = bernstein(coords[1])
    value_z, slope_z = bernstein(coords[2])
    place = iota((16, count), 0)
    at_y, at_z = place // 4, place % 4
    value_y, slope_y = pick(at_y, value_y), pick(at_y, slope_y)
    value_z, slope_z = pick(at_z, value_z), pick(at_z, slope_z)
    plain, with_y, with_z = value_y * value_z, slope_y * value_z, value_y * slope_z
    point = []
    for base in (0, 64):
        parts = [columns[base + 16 * i:base + 16 * i + 16] for i in range(4)]
        value = parts[0] * value_x[0] + parts[1] * value_x[1] + parts[2] * value_x[2] + parts[3] * value_x[3]
        slope = parts[0] * slope_x[0] + parts[1] * slope_x[1] + parts[2] * slope_x[2] + parts[3] * slope_x[3]
        products = (value * plain, slope * plain, value * with_y, value * with_z)
        point.append([jnp.sum(product, 0, keepdims=True) for product in products])
    (u, ux, uy, uz), (w, wx, wy, wz) = point
    nx, ny, nz = normals
    squared = nx * nx + ny * ny + nz * nz
    inner = ux * wx + uy * wy + uz * wz
    along_u = ux * nx + uy * ny + uz * nz
    along_w = wx * nx + wy * ny + wz * nz
    return squared * inner - 2.0 * along_u * along_w + PENALTY * squared * u * w


def spline(param):
    scaled = param * (CTRL - 3.0)
    start = jnp.clip(jnp.floor(scaled), 0.0, CTRL - 4.0)
    x = scaled - start
    c = 1.0 - x
    square, cube = x * x, x * x * x
    weights = (
        c * c * c / 6.0,
        (3.0 * cube - 6.0 * square + 4.0) / 6.0,
        (-3.0 * cube + 3.0 * square + 3.0 * x + 1.0) / 6.0,
        cube / 6.0,
    )
    offset = iota((CTRL, param.shape[1]), 0) - start.astype(I32)
    result = jnp.where(offset == 3, weights[3], 0.0)
    for k in (2, 1, 0):
        result = jnp.where(offset == k, weights[k], result)
    return result


def kernel(
    far_geom, block, far_cell, far_patch, near_geom, near_cell, near_patch, adjacency, fields,
    sine, sine_pair, total_pair, spread0, spread1, first, lane_power, pair_first, pair_power,
    far_out, design_out,
    rows, left, right, cells_v, cells_s, dens, ask, asked, reply, replied, grid, grids, part, parts,
    line, lines, edges, all_edges, halo, halo_rows, halo_cols,
    vol_send, vol_recv, dsg_send, dsg_recv, local_sem,
):
    me_vol = lax.axis_index("vol")
    me_dsg = lax.axis_index("dsg")
    far_count = far_geom.shape[1]
    near_count = near_geom.shape[1]

    barrier = pltpu.get_barrier_semaphore()

    def greet_vol(t, carry):
        peer = lax.rem(me_vol + t, VOL)
        pl.semaphore_signal(barrier, inc=1, device_id={"vol": peer}, device_id_type=MESH)
        return carry

    lax.fori_loop(1, VOL, greet_vol, 0)
    for t in range(1, DSG):
        peer = lax.rem(me_dsg + t, DSG)
        pl.semaphore_signal(barrier, inc=1, device_id={"dsg": peer}, device_id_type=MESH)

    def vol_copy(phase, source, target, t, at):
        peer = lax.rem(me_vol + t, VOL)
        return pltpu.make_async_remote_copy(
            src_ref=source(peer),
            dst_ref=target.at[at],
            send_sem=vol_send.at[phase, peer],
            recv_sem=vol_recv.at[phase, at],
            device_id={"vol": peer},
            device_id_type=MESH,
        )

    def vol_start(phase, source, target):
        def step(t, carry):
            vol_copy(phase, source, target, t, me_vol).start()
            return carry

        lax.fori_loop(1, VOL, step, 0)

    def vol_wait(phase, source, target):
        def step(t, carry):
            vol_copy(phase, source, target, t, lax.rem(me_vol + t, VOL)).wait()
            return carry

        lax.fori_loop(1, VOL, step, 0)

    def dsg_copy(phase, source, target, t, at):
        peer = lax.rem(me_dsg + t, DSG)
        return pltpu.make_async_remote_copy(
            src_ref=source(peer),
            dst_ref=target.at[at],
            send_sem=dsg_send.at[phase, peer],
            recv_sem=dsg_recv.at[phase, at],
            device_id={"dsg": peer},
            device_id_type=MESH,
        )

    def dsg_start(phase, source, target):
        for t in range(1, DSG):
            dsg_copy(phase, source, target, t, me_dsg).start()

    def dsg_wait(phase, source, target):
        for t in range(1, DSG):
            dsg_copy(phase, source, target, t, lax.rem(me_dsg + t, DSG)).wait()

    unseen = jnp.int32(PATCHES)
    near_ids, far_ids = near_patch[...], far_patch[...]
    ids = []
    previous = None
    for _ in range(GROUP):
        if previous is None:
            near_left, far_left = near_ids, far_ids
        else:
            near_left = jnp.where(near_ids > previous, near_ids, unseen)
            far_left = jnp.where(far_ids > previous, far_ids, unseen)
        previous = jnp.minimum(
            jnp.min(near_left, 1, keepdims=True), jnp.min(far_left, 1, keepdims=True)
        )
        ids.append(previous)

    to_block = iota((VOL, far_count), 0) == block[...]
    to_block_f = jnp.where(to_block, 1.0, 0.0)
    to_block_b = to_block_f.astype(BF16)
    earlier = jnp.where(
        iota((far_count, far_count), 0) < iota((far_count, far_count), 1), 1.0, 0.0
    ).astype(BF16)
    rank = jnp.sum(mm(to_block_b, earlier) * to_block_f, 0, keepdims=True).astype(I32)
    values = jnp.concatenate(
        [far_cell[...].astype(F32), far_geom[0:6, :], jnp.zeros((1, far_count), F32)], 0
    )
    placed = [jnp.where(rank == r, values, 0.0) for r in range(CAP)]
    placed.append(jnp.zeros((2 * LANES - 8 * CAP, far_count), F32))
    request = exact(mm_nt, to_block_b, jnp.concatenate(placed, 0))
    lane = iota((VOL, 2 * LANES), 1)
    for s in range(GROUP):
        request = jnp.where(lane == 8 * CAP + s, ids[s].astype(F32), request)
    ask[:, 0, :] = request
    asked[pl.ds(me_vol, 1)] = ask[pl.ds(me_vol, 1)]

    pl.semaphore_wait(barrier, VOL - 1 + DSG - 1)
    vol_start(0, lambda peer: ask.at[peer], asked)

    def take(cells, t, bounded=False):
        for r in range(LANES):
            cell = jnp.clip(cells[t, r], 0, fields.shape[0] - 1) if bounded else cells[t, r]
            rows[r:r + 1, :] = fields[pl.ds(cell, 1), :]
        return rows[...].T

    def scatter(at, strength, s_param, t_param, patch):
        left[:, pl.ds(at, LANES)] = spline(s_param)
        weights = spline(t_param) * strength
        for s in range(GROUP):
            right[s * CTRL:(s + 1) * CTRL, pl.ds(at, LANES)] = jnp.where(patch == ids[s], weights, 0.0)

    def near_chunk(t, carry):
        at = pl.multiple_of(t * LANES, LANES)
        columns = take(near_cell, t)
        geom = near_geom[:, pl.ds(at, LANES)]
        strength = densities(
            columns, [geom[i:i + 1] for i in range(3)], [geom[i:i + 1] for i in range(3, 6)]
        )
        scatter(at, strength, geom[6:7], geom[7:8], near_patch[:, pl.ds(at, LANES)])
        return carry

    chunks = near_count // LANES
    lax.fori_loop(0, chunks // 2, near_chunk, 0)

    vol_wait(0, lambda peer: ask.at[peer], asked)
    wanted = asked[:, 0, :].T
    tiles = []
    for t in range(CAP // 2):
        one = wanted[16 * t:16 * t + 8]
        two = wanted[16 * t + 8:16 * t + 16]
        tiles.append(jnp.concatenate([one, two], 1))
    cells_v[...] = jnp.concatenate(
        [jnp.clip((tile[0:1] + 0.5).astype(I32), 0, fields.shape[0] - 1) for tile in tiles] + [jnp.zeros((16 - CAP // 2, LANES), I32)], 0
    )
    to_scalar = pltpu.make_async_copy(cells_v, cells_s, local_sem)
    to_scalar.start()
    to_scalar.wait()
    dens[...] = jnp.zeros((LANES, LANES), F32)
    for t in range(CAP // 2):
        columns = take(cells_s, t, True)
        tile = tiles[t]
        strength = densities(
            columns, [tile[i:i + 1] for i in range(1, 4)], [tile[i:i + 1] for i in range(4, 7)]
        )
        dens[2 * t:2 * t + 1, 0:VOL] = strength[:, 0:VOL]
        dens[2 * t + 1:2 * t + 2, 0:VOL] = strength[:, VOL:]
    reply[:, 0, :] = dens[...].T[0:VOL, :]
    replied[pl.ds(me_vol, 1)] = reply[pl.ds(me_vol, 1)]
    vol_start(1, lambda peer: reply.at[peer], replied)

    lax.fori_loop(chunks // 2, chunks, near_chunk, 0)

    vol_wait(1, lambda peer: reply.at[peer], replied)
    answers = replied[:, 0, :].T
    high, middle, low = split3(answers)
    by_rank = mm(high, to_block_b) + mm(middle, to_block_b) + mm(low, to_block_b)
    far_strength = jnp.sum(
        jnp.where(iota((LANES, far_count), 0) == rank, by_rank, 0.0), 0, keepdims=True
    )
    far_out[...] = far_strength
    for t in range(far_count // LANES):
        at = slice(t * LANES, (t + 1) * LANES)
        scatter(
            near_count + t * LANES, far_strength[:, at], far_geom[6:7, at], far_geom[7:8, at], far_patch[:, at]
        )
    grid[:, 0, :] = dot3(mm_nt, left[...], right[...])
    grids[pl.ds(me_vol, 1)] = grid[pl.ds(me_vol, 1)]
    vol_start(2, lambda peer: grid.at[peer], grids)
    vol_wait(2, lambda peer: grid.at[peer], grids)

    got = grids[:, 0, :]
    patch_of = iota((PATCHES, VOL), 0).astype(F32)
    total = None
    for s in range(GROUP):
        place = jnp.where(patch_of == wanted[8 * CAP + s:8 * CAP + s + 1, :], 1.0, 0.0)
        term = exact(mm, place, got[:, s * CTRL:(s + 1) * CTRL])
        total = term if total is None else total + term
    total = dot3(mm, total, sine[...])
    for owner in range(DSG):
        base = owner * OWN
        pair = jnp.concatenate([total[base:base + HALF], total[base + HALF:base + OWN]], 1)
        for t in range(HALF):
            part[owner, :, t * LANES:(t + 1) * LANES] = pair[t:t + 1]
    parts[pl.ds(me_dsg, 1)] = part[pl.ds(me_dsg, 1)]
    dsg_start(0, lambda peer: part.at[peer], parts)
    dsg_wait(0, lambda peer: part.at[peer], parts)
    line[...] = parts[0] + parts[1] + parts[2] + parts[3]
    lines[pl.ds(me_vol, 1)] = line[...][None]
    vol_start(3, lambda peer: line, lines)
    vol_wait(3, lambda peer: line, lines)

    whole = dot3(mm, sine[...], lines[:, 0, :])
    span = [whole[:, t * LANES:(t + 1) * LANES] for t in range(HALF)]
    across = dot3(mm, first[...], whole)
    row_parts = [[], [], []]
    col_parts = [[], [], []]
    stacked = jnp.concatenate([across[:, t * LANES:(t + 1) * LANES] * lane_power[...] for t in range(HALF)], 0)
    edges_rows = stacked.reshape(HALF, 8, LANES)
    along = jnp.concatenate([dot3(mm_nt, pair_first[...], span[t]) * pair_power[...] for t in range(HALF)], 0)
    edges_cols = along.reshape(HALF, 16, CTRL)
    row_sum = [None, None]
    col_sum = [[None, None], [None, None]]
    for n in range(3):
        for side in range(2):
            term = edges_rows[:, 2 * n + side, :]
            row_sum[side] = term if n == 0 else row_sum[side] + term
            at = n * 4 * CTRL + side * CTRL
            edges[0:HALF, at:at + CTRL] = row_sum[side][:, 0:CTRL]
            edges[HALF:OWN, at:at + CTRL] = row_sum[side][:, CTRL:]
            for half in range(2):
                term = edges_cols[:, 6 * half + 2 * n + side, :]
                col_sum[half][side] = term if n == 0 else col_sum[half][side] + term
                at = n * 4 * CTRL + (2 + side) * CTRL
                edges[half * HALF:(half + 1) * HALF, at:at + CTRL] = col_sum[half][side]
    all_edges[pl.ds(me_dsg, 1)] = edges[...][None]
    dsg_start(1, lambda peer: edges, all_edges)
    dsg_wait(1, lambda peer: edges, all_edges)

    base = all_edges[...].reshape(PATCHES, 12 * CTRL)
    facing = [
        jnp.where(iota((PATCHES, PATCHES), 1) == adjacency[:, side:side + 1], 1.0, 0.0) for side in range(4)
    ]

    def exchange(edge):
        taken = []
        for side in range(4):
            other = side ^ 1
            taken.append(exact(mm, facing[side], edge[:, other * CTRL:(other + 1) * CTRL]))
        return jnp.concatenate(taken, 1)

    width = 4 * CTRL
    halo0 = exchange(base[:, 0:width])
    halo1 = exchange(base[:, width:2 * width] + dot3(mm, halo0, spread0[...]))
    halo2 = exchange(
        base[:, 2 * width:] + dot3(mm, halo0, spread1[...]) + dot3(mm, halo1, spread0[...])
    )
    halo[0], halo[1], halo[2] = halo0, halo1, halo2
    halo_rows[...] = jnp.zeros((HALF, 8, LANES), F32)
    halo_cols[...] = jnp.zeros((HALF, 16, CTRL), F32)
    mine = pl.ds(pl.multiple_of(me_dsg * OWN, 8), OWN)
    for k in range(3):
        own = halo[2 - k, mine, :]
        for side in range(2):
            row = 2 * k + side
            at = side * CTRL
            pair = jnp.concatenate([own[0:HALF, at:at + CTRL], own[HALF:OWN, at:at + CTRL]], 1)
            halo_rows[:, row, :] = pair * (SMOOTHING * lane_power[row:row + 1, :])
            at = (2 + side) * CTRL
            for half in range(2):
                halo_cols[:, 6 * half + row, :] = own[half * HALF:(half + 1) * HALF, at:at + CTRL] * (
                    SMOOTHING * pair_power[row:row + 1, :]
                )
    outcome = []
    for t in range(HALF):
        change = dot3(mm_tn, first[...], halo_rows[t]) + dot3(mm_tn, halo_cols[t], pair_first[...])
        outcome.append(span[t] * total_pair[...] + change)
    outcome = dot3(mm, jnp.concatenate(outcome, 0), sine_pair[...])
    for t in range(HALF):
        tile = dot3(mm, sine[...], outcome[t * CTRL:(t + 1) * CTRL])
        design_out[t] = tile[:, 0:CTRL]
        design_out[t + HALF] = tile[:, CTRL:]


def per_device(
    fields, far_geom, far_block, far_cell, far_patch, near_geom, near_cell, near_patch, adjacency
):
    far_count = far_cell.shape[0]
    near_count = near_cell.shape[0]
    points = far_count + near_count
    vmem = pl.BlockSpec(memory_space=pltpu.VMEM)
    smem = pl.BlockSpec(memory_space=pltpu.SMEM)
    tables = [jnp.asarray(t) for t in constants()]
    far, design = pl.pallas_call(
        kernel,
        out_shape=(
            jax.ShapeDtypeStruct((1, far_count), F32),
            jax.ShapeDtypeStruct((OWN, CTRL, CTRL), F32),
        ),
        in_specs=[vmem] * 5 + [smem] + [vmem] * (3 + len(tables)),
        out_specs=(vmem, vmem),
        scratch_shapes=[
            pltpu.VMEM((LANES, LANES), F32),
            pltpu.VMEM((CTRL, points), F32),
            pltpu.VMEM((GROUP * CTRL, points), F32),
            pltpu.VMEM((16, LANES), I32),
            pltpu.SMEM((16, LANES), I32),
            pltpu.VMEM((LANES, LANES), F32),
            pltpu.VMEM((VOL, 1, 2 * LANES), F32),
            pltpu.VMEM((VOL, 1, 2 * LANES), F32),
            pltpu.VMEM((VOL, 1, LANES), F32),
            pltpu.VMEM((VOL, 1, LANES), F32),
            pltpu.VMEM((VOL, 1, GROUP * CTRL), F32),
            pltpu.VMEM((VOL, 1, GROUP * CTRL), F32),
            pltpu.VMEM((DSG, 1, ROW), F32),
            pltpu.VMEM((DSG, 1, ROW), F32),
            pltpu.VMEM((1, ROW), F32),
            pltpu.VMEM((VOL, 1, ROW), F32),
            pltpu.VMEM((OWN, 12 * CTRL), F32),
            pltpu.VMEM((DSG, OWN, 12 * CTRL), F32),
            pltpu.VMEM((3, PATCHES, 4 * CTRL), F32),
            pltpu.VMEM((HALF, 8, LANES), F32),
            pltpu.VMEM((HALF, 16, CTRL), F32),
            pltpu.SemaphoreType.DMA((4, VOL)),
            pltpu.SemaphoreType.DMA((4, VOL)),
            pltpu.SemaphoreType.DMA((2, DSG)),
            pltpu.SemaphoreType.DMA((2, DSG)),
            pltpu.SemaphoreType.DMA,
        ],
        compiler_params=pltpu.CompilerParams(
            collective_id=0, has_side_effects=True, vmem_limit_bytes=60000 * 1024
        ),
    )(
        far_geom,
        far_block.reshape(1, far_count),
        far_cell.reshape(1, far_count),
        far_patch.reshape(1, far_count),
        near_geom,
        near_cell.reshape(near_count // LANES, LANES),
        near_patch.reshape(1, near_count),
        adjacency,
        fields,
        *tables,
    )
    return far.reshape(far_count), design


def solution(mesh):
    return jax.shard_map(
        per_device,
        mesh=mesh,
        in_specs=(
            P("vol", None),
            P(None, ("vol", "dsg")),
            P(("vol", "dsg"), None),
            P(("vol", "dsg")),
            P(("vol", "dsg")),
            P(None, ("vol", "dsg")),
            P(("vol", "dsg")),
            P(("vol", "dsg")),
            P(),
        ),
        out_specs=(P(("vol", "dsg")), P("dsg", None, None)),
        check_vma=False,
    )
```

time: 609 us -> 77.7 us (0.13); the launches traced: 598 us -> 77.4 us
  waiting for transfers between devices: 274 us -> 0 us
  local copies, waits for them, and re-layouts: 155 us -> 4.74 us
  other arithmetic: 114 us -> 0 us
  Pallas kernels: 0 us -> 72.1 us
  starting transfers between devices: 24 us -> 0 us
  between operations: 20.4 us -> 0.64 us
  matrix products: 10.6 us -> 0 us
    psum x1 -> x0, waiting for transfers between devices: 256 us -> none  [per_device(): lax.psum(grid_whole, ('vol', 'dsg')).reshape(patches, control, control)]
    pallas_call x0 -> x1, Pallas kernels: none -> 72.1 us  [per_device(): pl.pallas_call(kernel, out_shape=(jax.ShapeDtypeStruct((1, far_count), F3...]
    sub x41 -> x0, other arithmetic: 51.5 us -> none  [the longest x37 42 us: precondition(): lax.linalg.tridiagonal_solve(below_diag, main_diag, above_diag, residual)]
    mul x45 -> x0, local copies, waits for them, and re-layouts: 47.1 us -> none  [the longest x16 47 us: tensor_basis(): factor_x[:, None, None, :] * factor_y[None, :, None, :]]
    concatenate x3 -> x0, local copies, waits for them, and re-layouts: 35.3 us -> none  [precondition(): lax.linalg.tridiagonal_solve(below_diag, main_diag, above_diag, residual)]
    all_to_all x2 -> x0, starting transfers between devices: 23.6 us -> none  [the longest x1 13.2 us: per_device(): lax.all_to_all(request, 'vol', split_axis=1, concat_axis=1, tiled=True)]
    scatter x17 -> x0, local copies, waits for them, and re-layouts: 18.3 us -> none  [the longest x3 6.61 us: apply_operator(): padded = padded.at[:, 0, 1:-1].set(halo_rows[:, 0])]
    all_to_all x2 -> x0, waiting for transfers between devices: 17.6 us -> none  [the longest x1 17.6 us: per_device(): lax.all_to_all(picked, 'vol', split_axis=1, concat_axis=1, tiled=True)]
  transfers between devices with their start and end apart: 3 -> 0, of which waited for: 2 -> 0; matrix products, arithmetic and copies ran while one was open for 13% -> 0% of each run, Pallas kernels for 0% -> 0%
where the time goes in v1:
time: 77.7 us; the launch traced here: 77.4 us
  Pallas kernels  72.1 us (93%)
  local copies, waits for them, and re-layouts  4.74 us (6%)
    pallas_call x1, Pallas kernels, per_device(): pl.pallas_call(kernel, out_shape=(jax.ShapeDtypeStruct((1, far_count), F3...  72.1 us
    unnamed x3, local copies, waits for them, and re-layouts  4.74 us

profile of v1, /device:TPU:1, one launch (start us, length us, event | category | flops | bytes accessed | tf_op | source)
XLA Modules:
  0.0 77.4 jit_solution(6025827206625345395)
XLA Ops:
  0.6 1.4 %copy.20.adjacency = s32[96,4]{1,0:T(8,128)} copy(s32[96,4]{0,1:T(4,128)} %param.26) | data formatting | bytes 3072 | tf_op args[8]
  2.0 72.1 %shard_map.185 = (f32[1,512]{1,0:T(1,128)}, f32[24,64,64]{2,1,0:T(8,128)}) custom-call(f32[8,512]{1,0:T(8,128)} %far_geom.1, s32[1,512]{1,0:T(1,128)} %bitcast.8, s32[1,512]{1,0:T(1,128)} %bitcast.9, s32[1,512]{1,0:T(1,128)} %bitcast.10, f32[8,2048]{1,0:T(8,128)} %near_geom.1, s32[16,128]{1,0:T(8,128)} %bitcast.6, s32[1,2048]{1,0:T(1,128)} %bitcast.7, ...), custom_call_target="tpu_custom_call" | custom-call | tf_op jit(solution)/shard_map/pallas_call | solution.py:449
  74.1 1.3 %copy.23 = f32[512]{0:T(512)} copy(f32[512]{0:T(512)} %bitcast.11) | data formatting | bytes 4096
  75.4 2.1 %copy.24 = f32[24,64,64]{2,1,0:T(8,128)} copy(f32[24,64,64]{2,1,0:T(8,128)} %get-tuple-element.9) | data formatting | bytes 786432

commit v2 on v1

--- a/solution.py
+++ b/solution.py
@@ -18,6 +18,9 @@
 SMOOTHING = 16.0
 LANES = 128
 VOL = 64
+VOL_Z = 8
+VOL_Y = 4
+VOL_C = 2
 DSG = 4
 PATCHES = 96
 OWN = PATCHES // DSG
@@ -168,73 +171,88 @@
 
 
 def kernel(
-    far_geom, block, far_cell, far_patch, near_geom, near_cell, near_patch, adjacency, fields,
-    sine, sine_pair, total_pair, spread0, spread1, first, lane_power, pair_first, pair_power,
+    far_geom, block, far_cell, far_patch, near_geom, near_cell, near_patch, adjacency,
+    fields_in, sine_in, sine_pair_in, total_pair_in, spread0_in, spread1_in, first_in, lane_power_in,
+    pair_first_in, pair_power_in,
     far_out, design_out,
+    fields, sine, sine_pair, total_pair, spread0, spread1, first, lane_power, pair_first, pair_power,
     rows, left, right, cells_v, cells_s, dens, ask, asked, reply, replied, grid, grids, part, parts,
     line, lines, edges, all_edges, halo, halo_rows, halo_cols,
-    vol_send, vol_recv, dsg_send, dsg_recv, local_sem,
+    vol_send, vol_recv, dsg_send, dsg_recv, z_send, z_recv, y_send, y_recv, core_send, core_recv,
+    local_sem, load_sem, fields_sem,
 ):
     me_vol = lax.axis_index("vol")
     me_dsg = lax.axis_index("dsg")
     far_count = far_geom.shape[1]
     near_count = near_geom.shape[1]
 
+    load_fields = pltpu.make_async_copy(fields_in, fields, fields_sem)
+    load_fields.start()
+    loads = [
+        pltpu.make_async_copy(source, target, load_sem.at[i])
+        for i, (source, target) in enumerate(
+            (
+                (sine_in, sine), (sine_pair_in, sine_pair), (total_pair_in, total_pair),
+                (spread0_in, spread0), (spread1_in, spread1), (first_in, first),
+                (lane_power_in, lane_power), (pair_first_in, pair_first), (pair_power_in, pair_power),
+            )
+        )
+    ]
+    for load in loads:
+        load.start()
+
     barrier = pltpu.get_barrier_semaphore()
 
     def greet_vol(t, carry):
-        peer = lax.rem(me_vol + t, VOL)
+        peer = jnp.where(me_vol + t >= VOL, me_vol + t - VOL, me_vol + t)
         pl.semaphore_signal(barrier, inc=1, device_id={"vol": peer}, device_id_type=MESH)
         return carry
 
     lax.fori_loop(1, VOL, greet_vol, 0)
     for t in range(1, DSG):
-        peer = lax.rem(me_dsg + t, DSG)
+        peer = jnp.where(me_dsg + t >= DSG, me_dsg + t - DSG, me_dsg + t)
         pl.semaphore_signal(barrier, inc=1, device_id={"dsg": peer}, device_id_type=MESH)
 
-    def vol_copy(phase, source, target, t, at):
-        peer = lax.rem(me_vol + t, VOL)
-        return pltpu.make_async_remote_copy(
-            src_ref=source(peer),
-            dst_ref=target.at[at],
-            send_sem=vol_send.at[phase, peer],
-            recv_sem=vol_recv.at[phase, at],
-            device_id={"vol": peer},
-            device_id_type=MESH,
-        )
+    def wrap(index, size):
+        return jnp.where(index >= size, index - size, index)
 
     def vol_start(phase, source, target):
         def step(t, carry):
-            vol_copy(phase, source, target, t, me_vol).start()
+            peer = wrap(me_vol + t, VOL)
+            pltpu.make_async_remote_copy(
+                src_ref=source.at[peer],
+                dst_ref=target.at[me_vol],
+                send_sem=vol_send.at[phase],
+                recv_sem=vol_recv.at[phase],
+                device_id={"vol": peer},
+                device_id_type=MESH,
+            ).start()
             return carry
 
         lax.fori_loop(1, VOL, step, 0)
 
+    def settle(ref, sem):
+        pltpu.make_async_copy(ref, ref, sem).wait()
+
     def vol_wait(phase, source, target):
-        def step(t, carry):
-            vol_copy(phase, source, target, t, lax.rem(me_vol + t, VOL)).wait()
-            return carry
-
-        lax.fori_loop(1, VOL, step, 0)
-
-    def dsg_copy(phase, source, target, t, at):
-        peer = lax.rem(me_dsg + t, DSG)
-        return pltpu.make_async_remote_copy(
-            src_ref=source(peer),
-            dst_ref=target.at[at],
-            send_sem=dsg_send.at[phase, peer],
-            recv_sem=dsg_recv.at[phase, at],
-            device_id={"dsg": peer},
-            device_id_type=MESH,
-        )
+        settle(target.at[pl.ds(0, VOL - 1)], vol_recv.at[phase])
+        settle(source.at[pl.ds(0, VOL - 1)], vol_send.at[phase])
 
     def dsg_start(phase, source, target):
         for t in range(1, DSG):
-            dsg_copy(phase, source, target, t, me_dsg).start()
-
-    def dsg_wait(phase, source, target):
-        for t in range(1, DSG):
-            dsg_copy(phase, source, target, t, lax.rem(me_dsg + t, DSG)).wait()
+            peer = wrap(me_dsg + t, DSG)
+            pltpu.make_async_remote_copy(
+                src_ref=source(peer),
+                dst_ref=target.at[me_dsg],
+                send_sem=dsg_send.at[phase],
+                recv_sem=dsg_recv.at[phase],
+                device_id={"dsg": peer},
+                device_id_type=MESH,
+            ).start()
+
+    def dsg_wait(phase, target):
+        settle(target.at[pl.ds(0, DSG - 1)], dsg_recv.at[phase])
+        settle(target.at[pl.ds(0, DSG - 1)], dsg_send.at[phase])
 
     unseen = jnp.int32(PATCHES)
     near_ids, far_ids = near_patch[...], far_patch[...]
@@ -270,8 +288,14 @@
     ask[:, 0, :] = request
     asked[pl.ds(me_vol, 1)] = ask[pl.ds(me_vol, 1)]
 
+    sides = jnp.concatenate(
+        [jnp.concatenate([adjacency[...], jnp.full((4, LANES - PATCHES), -1, I32)], 1)] * 2, 0
+    ).astype(F32).T[0:PATCHES]
+    patch_lane = iota((PATCHES, PATCHES), 1).astype(F32)
+    facing = [jnp.where(patch_lane == sides[:, side:side + 1], 1.0, 0.0).astype(BF16) for side in range(4)]
+
     pl.semaphore_wait(barrier, VOL - 1 + DSG - 1)
-    vol_start(0, lambda peer: ask.at[peer], asked)
+    vol_start(0, ask, asked)
 
     def take(cells, t, bounded=False):
         for r in range(LANES):
@@ -295,10 +319,11 @@
         scatter(at, strength, geom[6:7], geom[7:8], near_patch[:, pl.ds(at, LANES)])
         return carry
 
+    load_fields.wait()
     chunks = near_count // LANES
     lax.fori_loop(0, chunks // 2, near_chunk, 0)
 
-    vol_wait(0, lambda peer: ask.at[peer], asked)
+    vol_wait(0, ask, asked)
     wanted = asked[:, 0, :].T
     tiles = []
     for t in range(CAP // 2):
@@ -322,11 +347,11 @@
         dens[2 * t + 1:2 * t + 2, 0:VOL] = strength[:, VOL:]
     reply[:, 0, :] = dens[...].T[0:VOL, :]
     replied[pl.ds(me_vol, 1)] = reply[pl.ds(me_vol, 1)]
-    vol_start(1, lambda peer: reply.at[peer], replied)
+    vol_start(1, reply, replied)
 
     lax.fori_loop(chunks // 2, chunks, near_chunk, 0)
 
-    vol_wait(1, lambda peer: reply.at[peer], replied)
+    vol_wait(1, reply, replied)
     answers = replied[:, 0, :].T
     high, middle, low = split3(answers)
     by_rank = mm(high, to_block_b) + mm(middle, to_block_b) + mm(low, to_block_b)
@@ -341,8 +366,8 @@
         )
     grid[:, 0, :] = dot3(mm_nt, left[...], right[...])
     grids[pl.ds(me_vol, 1)] = grid[pl.ds(me_vol, 1)]
-    vol_start(2, lambda peer: grid.at[peer], grids)
-    vol_wait(2, lambda peer: grid.at[peer], grids)
+    vol_start(2, grid, grids)
+    vol_wait(2, grid, grids)
 
     got = grids[:, 0, :]
     patch_of = iota((PATCHES, VOL), 0).astype(F32)
@@ -351,6 +376,7 @@
         place = jnp.where(patch_of == wanted[8 * CAP + s:8 * CAP + s + 1, :], 1.0, 0.0)
         term = exact(mm, place, got[:, s * CTRL:(s + 1) * CTRL])
         total = term if total is None else total + term
+    loads[0].wait()
     total = dot3(mm, total, sine[...])
     for owner in range(DSG):
         base = owner * OWN
@@ -359,13 +385,64 @@
             part[owner, :, t * LANES:(t + 1) * LANES] = pair[t:t + 1]
     parts[pl.ds(me_dsg, 1)] = part[pl.ds(me_dsg, 1)]
     dsg_start(0, lambda peer: part.at[peer], parts)
-    dsg_wait(0, lambda peer: part.at[peer], parts)
+    dsg_wait(0, parts)
     line[...] = parts[0] + parts[1] + parts[2] + parts[3]
-    lines[pl.ds(me_vol, 1)] = line[...][None]
-    vol_start(3, lambda peer: line, lines)
-    vol_wait(3, lambda peer: line, lines)
-
-    whole = dot3(mm, sine[...], lines[:, 0, :])
+    me_z, me_y, me_c = me_vol // (VOL_Y * VOL_C), me_vol // VOL_C % VOL_Y, me_vol % VOL_C
+
+    def at_vol(z, y, c):
+        return (z * VOL_Y + y) * VOL_C + c
+
+    lines[me_z, me_y, me_c] = line[...]
+    ring = (1, 7, 2, 6, 3, 5, 4)
+    for turn in ring:
+        pltpu.make_async_remote_copy(
+            src_ref=line,
+            dst_ref=lines.at[me_z, me_y, me_c],
+            send_sem=z_send,
+            recv_sem=z_recv.at[turn],
+            device_id={"vol": at_vol(wrap(me_z + turn, VOL_Z), me_y, me_c)},
+            device_id_type=MESH,
+        ).start()
+
+    def to_core(source, target):
+        pltpu.make_async_remote_copy(
+            src_ref=source,
+            dst_ref=target,
+            send_sem=core_send,
+            recv_sem=core_recv,
+            device_id={"vol": at_vol(me_z, me_y, 1 - me_c)},
+            device_id_type=MESH,
+        ).start()
+
+    for turn in (0,) + ring:
+        z = wrap(me_z + VOL_Z - turn, VOL_Z)
+        target = lines.at[z, me_y, me_c]
+        source = line if turn == 0 else target
+        if turn:
+            settle(target, z_recv.at[turn])
+        for step in (2, 1, 3):
+            pltpu.make_async_remote_copy(
+                src_ref=source,
+                dst_ref=target,
+                send_sem=y_send,
+                recv_sem=y_recv.at[step],
+                device_id={"vol": at_vol(me_z, wrap(me_y + step, VOL_Y), me_c)},
+                device_id_type=MESH,
+            ).start()
+        to_core(source, target)
+    for step in (1, 3, 2):
+        y = wrap(me_y + VOL_Y - step, VOL_Y)
+        column = lines.at[:, y, me_c]
+        settle(column, y_recv.at[step])
+        to_core(column, column)
+    settle(lines.at[:, :, 0], core_recv)
+    settle(lines.at[pl.ds(0, VOL_Z - 1), 0, 0], z_send)
+    settle(lines.at[:, pl.ds(0, VOL_Y - 1), 0], y_send)
+    settle(lines.at[:, :, 0], core_send)
+
+    for load in loads[1:]:
+        load.wait()
+    whole = dot3(mm, sine[...], lines[...].reshape(VOL, ROW))
     span = [whole[:, t * LANES:(t + 1) * LANES] for t in range(HALF)]
     across = dot3(mm, first[...], whole)
     row_parts = [[], [], []]
@@ -390,12 +467,14 @@
                 edges[half * HALF:(half + 1) * HALF, at:at + CTRL] = col_sum[half][side]
     all_edges[pl.ds(me_dsg, 1)] = edges[...][None]
     dsg_start(1, lambda peer: edges, all_edges)
-    dsg_wait(1, lambda peer: edges, all_edges)
+    calm = dot3(mm, jnp.concatenate([tile * total_pair[...] for tile in span], 0), sine_pair[...])
+    for t in range(HALF):
+        design_out[t] = dot3(mm, sine[...], calm[t * CTRL:(t + 1) * CTRL])
+    first_free = dot3(mm, first[...], sine[...])
+    pair_first_free = dot3(mm, pair_first[...], sine_pair[...])
+    dsg_wait(1, all_edges)
 
     base = all_edges[...].reshape(PATCHES, 12 * CTRL)
-    facing = [
-        jnp.where(iota((PATCHES, PATCHES), 1) == adjacency[:, side:side + 1], 1.0, 0.0) for side in range(4)
-    ]
 
     def exchange(edge):
         taken = []
@@ -426,15 +505,18 @@
                 halo_cols[:, 6 * half + row, :] = own[half * HALF:(half + 1) * HALF, at:at + CTRL] * (
                     SMOOTHING * pair_power[row:row + 1, :]
                 )
-    outcome = []
+    rows_free = dot3(mm, halo_rows[...].reshape(HALF * 8, LANES), sine_pair[...])
+    cols_free = dot3(mm, halo_cols[...].reshape(HALF * 16, CTRL), sine[...])
     for t in range(HALF):
-        change = dot3(mm_tn, first[...], halo_rows[t]) + dot3(mm_tn, halo_cols[t], pair_first[...])
-        outcome.append(span[t] * total_pair[...] + change)
-    outcome = dot3(mm, jnp.concatenate(outcome, 0), sine_pair[...])
-    for t in range(HALF):
-        tile = dot3(mm, sine[...], outcome[t * CTRL:(t + 1) * CTRL])
-        design_out[t] = tile[:, 0:CTRL]
-        design_out[t + HALF] = tile[:, CTRL:]
+        outer = jnp.concatenate([first_free, cols_free[t * 16:(t + 1) * 16]], 0)
+        inner = jnp.concatenate([rows_free[t * 8:(t + 1) * 8], pair_first_free], 0)
+        design_out[t] += dot3(mm_tn, outer, inner)
+
+
+def finish(far_ref, pair_ref, far_out, design_out):
+    far_out[...] = far_ref[...]
+    design_out[0:HALF] = pair_ref[:, :, 0:CTRL]
+    design_out[HALF:OWN] = pair_ref[:, :, CTRL:]
 
 
 def per_device(
@@ -445,16 +527,20 @@
     points = far_count + near_count
     vmem = pl.BlockSpec(memory_space=pltpu.VMEM)
     smem = pl.BlockSpec(memory_space=pltpu.SMEM)
+    stay = pl.BlockSpec(memory_space=pl.ANY)
     tables = [jnp.asarray(t) for t in constants()]
-    far, design = pl.pallas_call(
+    dma = pltpu.SemaphoreType.DMA
+    far, pairs = pl.pallas_call(
         kernel,
         out_shape=(
             jax.ShapeDtypeStruct((1, far_count), F32),
-            jax.ShapeDtypeStruct((OWN, CTRL, CTRL), F32),
+            jax.ShapeDtypeStruct((HALF, CTRL, LANES), F32),
         ),
-        in_specs=[vmem] * 5 + [smem] + [vmem] * (3 + len(tables)),
+        in_specs=[vmem] * 5 + [smem] + [vmem] * 2 + [stay] * (1 + len(tables)),
         out_specs=(vmem, vmem),
-        scratch_shapes=[
+        scratch_shapes=[pltpu.VMEM(fields.shape, F32)]
+        + [pltpu.VMEM(t.shape, F32) for t in tables]
+        + [
             pltpu.VMEM((LANES, LANES), F32),
             pltpu.VMEM((CTRL, points), F32),
             pltpu.VMEM((GROUP * CTRL, points), F32),
@@ -470,17 +556,15 @@
             pltpu.VMEM((DSG, 1, ROW), F32),
             pltpu.VMEM((DSG, 1, ROW), F32),
             pltpu.VMEM((1, ROW), F32),
-            pltpu.VMEM((VOL, 1, ROW), F32),
+            pltpu.VMEM((VOL_Z, VOL_Y, VOL_C, 1, ROW), F32),
             pltpu.VMEM((OWN, 12 * CTRL), F32),
             pltpu.VMEM((DSG, OWN, 12 * CTRL), F32),
             pltpu.VMEM((3, PATCHES, 4 * CTRL), F32),
             pltpu.VMEM((HALF, 8, LANES), F32),
             pltpu.VMEM((HALF, 16, CTRL), F32),
-            pltpu.SemaphoreType.DMA((4, VOL)),
-            pltpu.SemaphoreType.DMA((4, VOL)),
-            pltpu.SemaphoreType.DMA((2, DSG)),
-            pltpu.SemaphoreType.DMA((2, DSG)),
-            pltpu.SemaphoreType.DMA,
+            dma((3,)), dma((3,)), dma((2,)), dma((2,)),
+            dma, dma((VOL_Z,)), dma, dma((VOL_Y,)), dma, dma,
+            dma, dma((len(tables),)), dma,
         ],
         compiler_params=pltpu.CompilerParams(
             collective_id=0, has_side_effects=True, vmem_limit_bytes=60000 * 1024
@@ -493,10 +577,19 @@
         near_geom,
         near_cell.reshape(near_count // LANES, LANES),
         near_patch.reshape(1, near_count),
-        adjacency,
+        adjacency.T,
         fields,
         *tables,
     )
+    far, design = pl.pallas_call(
+        finish,
+        out_shape=(
+            jax.ShapeDtypeStruct((1, far_count), F32),
+            jax.ShapeDtypeStruct((OWN, CTRL, CTRL), F32),
+        ),
+        in_specs=[vmem] * 2,
+        out_specs=(vmem, vmem),
+    )(far, pairs)
     return far.reshape(far_count), design
 
 

time: 77.7 us -> 65.9 us (0.85)
  Pallas kernels: 72.1 us -> 65.1 us
  local copies, waits for them, and re-layouts: 4.74 us -> 0 us
    pallas_call x1, Pallas kernels: 72.1 us -> 63 us  [per_device(): pl.pallas_call(kernel, out_shape=(jax.ShapeDtypeStruct((1, far_count), F3...]
    unnamed x3 -> x0, local copies, waits for them, and re-layouts: 4.74 us -> none
    pallas_call x0 -> x1, Pallas kernels: none -> 2.05 us  [per_device(): pl.pallas_call(finish, out_shape=(jax.ShapeDtypeStruct((1, far_count), F3...]
where the time goes in v2:
time: 65.9 us; the launch traced here: 65.7 us
  Pallas kernels  65.1 us (99%)
    pallas_call x1, Pallas kernels, per_device(): pl.pallas_call(kernel, out_shape=(jax.ShapeDtypeStruct((1, far_count), F3...  63 us
    pallas_call x1, Pallas kernels, per_device(): pl.pallas_call(finish, out_shape=(jax.ShapeDtypeStruct((1, far_count), F3...  2.05 us

profile of v2, /device:TPU:1, one launch (start us, length us, event | category | flops | bytes accessed | tf_op | source)
XLA Modules:
  0.0 65.7 jit_solution(12607747686414484050)
XLA Ops:
  0.6 63.0 %shard_map.185 = (f32[1,512]{1,0:T(1,128)}, f32[12,64,128]{2,1,0:T(8,128)}) custom-call(f32[8,512]{1,0:T(8,128)} %far_geom.1, s32[1,512]{1,0:T(1,128)} %bitcast.9, s32[1,512]{1,0:T(1,128)} %bitcast.10, s32[1,512]{1,0:T(1,128)} %bitcast.11, f32[8,2048]{1,0:T(8,128)} %near_geom.1, s32[16,128]{1,0:T(8,128)} %bitcast.7, s32[1,2048]{1,0:T(1,128)} %bitcast.8, ...), custom_call_target="tpu_custom_call" | custom-call | tf_op jit(solution)/shard_map/pallas_call | solution.py:533
  63.7 2.0 %shard_map.186 = (f32[1,512]{1,0:T(1,128)}, f32[24,64,64]{2,1,0:T(8,128)}) custom-call(f32[1,512]{1,0:T(1,128)} %get-tuple-element.6.far_ref, f32[12,64,128]{2,1,0:T(8,128)} %get-tuple-element.7.pair_ref), custom_call_target="tpu_custom_call" | custom-call | tf_op jit(solution)/shard_map/pallas_call | solution.py:584

commit v3 on v2

--- a/solution.py
+++ b/solution.py
@@ -18,13 +18,15 @@
 SMOOTHING = 16.0
 LANES = 128
 VOL = 64
-VOL_Z = 8
-VOL_Y = 4
 VOL_C = 2
 DSG = 4
 PATCHES = 96
 OWN = PATCHES // DSG
 HALF = OWN // 2
+CHUNKS = 3
+TILES = HALF // CHUNKS
+PIECE = OWN // CHUNKS
+SPAN = TILES * LANES
 ROW = OWN * CTRL
 NOBODY = 999.0
 
@@ -68,7 +70,8 @@
             for half in range(2):
                 pair_first[6 * half + row, half * CTRL:(half + 1) * CTRL] = power[k] * ends[side]
                 pair_power[6 * half + row] = power[k]
-    tables = (sine, sine_pair, total_pair, spread(0), spread(1), first, lane_power, pair_first, pair_power)
+    by_core = np.concatenate([np.arange(core, VOL, VOL_C) for core in range(VOL_C)])
+    tables = (sine, sine[:, by_core], sine_pair, total_pair, spread(0), spread(1), first, lane_power, pair_first, pair_power)
     return [np.asarray(t, np.float32) for t in tables]
 
 
@@ -172,13 +175,13 @@
 
 def kernel(
     far_geom, block, far_cell, far_patch, near_geom, near_cell, near_patch, adjacency,
-    fields_in, sine_in, sine_pair_in, total_pair_in, spread0_in, spread1_in, first_in, lane_power_in,
+    fields_in, sine_in, sine_rows_in, sine_pair_in, total_pair_in, spread0_in, spread1_in, first_in, lane_power_in,
     pair_first_in, pair_power_in,
     far_out, design_out,
-    fields, sine, sine_pair, total_pair, spread0, spread1, first, lane_power, pair_first, pair_power,
+    fields, sine, sine_rows, sine_pair, total_pair, spread0, spread1, first, lane_power, pair_first, pair_power,
     rows, left, right, cells_v, cells_s, dens, ask, asked, reply, replied, grid, grids, part, parts,
     line, lines, edges, all_edges, halo, halo_rows, halo_cols,
-    vol_send, vol_recv, dsg_send, dsg_recv, z_send, z_recv, y_send, y_recv, core_send, core_recv,
+    vol_send, vol_recv, dsg_send, dsg_recv, row_send, row_recv, core_send, core_recv,
     local_sem, load_sem, fields_sem,
 ):
     me_vol = lax.axis_index("vol")
@@ -192,7 +195,7 @@
         pltpu.make_async_copy(source, target, load_sem.at[i])
         for i, (source, target) in enumerate(
             (
-                (sine_in, sine), (sine_pair_in, sine_pair), (total_pair_in, total_pair),
+                (sine_in, sine), (sine_rows_in, sine_rows), (sine_pair_in, sine_pair), (total_pair_in, total_pair),
                 (spread0_in, spread0), (spread1_in, spread1), (first_in, first),
                 (lane_power_in, lane_power), (pair_first_in, pair_first), (pair_power_in, pair_power),
             )
@@ -239,7 +242,7 @@
         settle(source.at[pl.ds(0, VOL - 1)], vol_send.at[phase])
 
     def dsg_start(phase, source, target):
-        for t in range(1, DSG):
+        for t in (2, 1, 3):
             peer = wrap(me_dsg + t, DSG)
             pltpu.make_async_remote_copy(
                 src_ref=source(peer),
@@ -294,24 +297,24 @@
     patch_lane = iota((PATCHES, PATCHES), 1).astype(F32)
     facing = [jnp.where(patch_lane == sides[:, side:side + 1], 1.0, 0.0).astype(BF16) for side in range(4)]
 
-    pl.semaphore_wait(barrier, VOL - 1 + DSG - 1)
-    vol_start(0, ask, asked)
-
-    def take(cells, t, bounded=False):
+
+    def take(cells, t, slot, bounded=False):
         for r in range(LANES):
             cell = jnp.clip(cells[t, r], 0, fields.shape[0] - 1) if bounded else cells[t, r]
-            rows[r:r + 1, :] = fields[pl.ds(cell, 1), :]
-        return rows[...].T
+            rows[slot, r:r + 1, :] = fields[pl.ds(cell, 1), :]
+        return rows[slot].T
 
     def scatter(at, strength, s_param, t_param, patch):
         left[:, pl.ds(at, LANES)] = spline(s_param)
-        weights = spline(t_param) * strength
+        weights = spline(t_param)
+        if strength is not None:
+            weights = weights * strength
         for s in range(GROUP):
             right[s * CTRL:(s + 1) * CTRL, pl.ds(at, LANES)] = jnp.where(patch == ids[s], weights, 0.0)
 
     def near_chunk(t, carry):
         at = pl.multiple_of(t * LANES, LANES)
-        columns = take(near_cell, t)
+        columns = take(near_cell, t, 0)
         geom = near_geom[:, pl.ds(at, LANES)]
         strength = densities(
             columns, [geom[i:i + 1] for i in range(3)], [geom[i:i + 1] for i in range(3, 6)]
@@ -321,7 +324,11 @@
 
     load_fields.wait()
     chunks = near_count // LANES
-    lax.fori_loop(0, chunks // 2, near_chunk, 0)
+    lax.fori_loop(0, chunks // 4, near_chunk, 0)
+
+    pl.semaphore_wait(barrier, VOL - 1 + DSG - 1)
+    vol_start(0, ask, asked)
+    lax.fori_loop(chunks // 4, 5 * chunks // 8, near_chunk, 0)
 
     vol_wait(0, ask, asked)
     wanted = asked[:, 0, :].T
@@ -338,7 +345,7 @@
     to_scalar.wait()
     dens[...] = jnp.zeros((LANES, LANES), F32)
     for t in range(CAP // 2):
-        columns = take(cells_s, t, True)
+        columns = take(cells_s, t, t % 4, True)
         tile = tiles[t]
         strength = densities(
             columns, [tile[i:i + 1] for i in range(1, 4)], [tile[i:i + 1] for i in range(4, 7)]
@@ -349,8 +356,18 @@
     replied[pl.ds(me_vol, 1)] = reply[pl.ds(me_vol, 1)]
     vol_start(1, reply, replied)
 
-    lax.fori_loop(chunks // 2, chunks, near_chunk, 0)
-
+    lax.fori_loop(5 * chunks // 8, chunks, near_chunk, 0)
+    near_grid = dot3(mm_nt, left[:, 0:near_count], right[:, 0:near_count])
+
+    for t in range(far_count // LANES):
+        at = slice(t * LANES, (t + 1) * LANES)
+        scatter(near_count + t * LANES, None, far_geom[6:7, at], far_geom[7:8, at], far_patch[:, at])
+    far_right, far_right_low = split2(right[:, near_count:])
+    patch_of = iota((PATCHES, VOL), 0).astype(F32)
+    places = [
+        jnp.where(patch_of == wanted[8 * CAP + s:8 * CAP + s + 1, :], 1.0, 0.0).astype(BF16)
+        for s in range(GROUP)
+    ]
     vol_wait(1, reply, replied)
     answers = replied[:, 0, :].T
     high, middle, low = split3(answers)
@@ -359,122 +376,116 @@
         jnp.where(iota((LANES, far_count), 0) == rank, by_rank, 0.0), 0, keepdims=True
     )
     far_out[...] = far_strength
-    for t in range(far_count // LANES):
-        at = slice(t * LANES, (t + 1) * LANES)
-        scatter(
-            near_count + t * LANES, far_strength[:, at], far_geom[6:7, at], far_geom[7:8, at], far_patch[:, at]
-        )
-    grid[:, 0, :] = dot3(mm_nt, left[...], right[...])
+    far_left, far_left_low = split2(left[:, near_count:] * far_strength)
+    grid[:, 0, :] = (
+        near_grid
+        + mm_nt(far_left, far_right)
+        + mm_nt(far_left, far_right_low)
+        + mm_nt(far_left_low, far_right)
+    )
     grids[pl.ds(me_vol, 1)] = grid[pl.ds(me_vol, 1)]
     vol_start(2, grid, grids)
     vol_wait(2, grid, grids)
 
     got = grids[:, 0, :]
-    patch_of = iota((PATCHES, VOL), 0).astype(F32)
     total = None
     for s in range(GROUP):
-        place = jnp.where(patch_of == wanted[8 * CAP + s:8 * CAP + s + 1, :], 1.0, 0.0)
-        term = exact(mm, place, got[:, s * CTRL:(s + 1) * CTRL])
+        term = exact(mm, places[s], got[:, s * CTRL:(s + 1) * CTRL])
         total = term if total is None else total + term
     loads[0].wait()
     total = dot3(mm, total, sine[...])
     for owner in range(DSG):
         base = owner * OWN
-        pair = jnp.concatenate([total[base:base + HALF], total[base + HALF:base + OWN]], 1)
         for t in range(HALF):
-            part[owner, :, t * LANES:(t + 1) * LANES] = pair[t:t + 1]
+            low = base + t // TILES * PIECE + t % TILES
+            part[owner, :, t * LANES:t * LANES + CTRL] = total[low:low + 1]
+            part[owner, :, t * LANES + CTRL:(t + 1) * LANES] = total[low + TILES:low + TILES + 1]
     parts[pl.ds(me_dsg, 1)] = part[pl.ds(me_dsg, 1)]
     dsg_start(0, lambda peer: part.at[peer], parts)
     dsg_wait(0, parts)
-    line[...] = parts[0] + parts[1] + parts[2] + parts[3]
-    me_z, me_y, me_c = me_vol // (VOL_Y * VOL_C), me_vol // VOL_C % VOL_Y, me_vol % VOL_C
-
-    def at_vol(z, y, c):
-        return (z * VOL_Y + y) * VOL_C + c
-
-    lines[me_z, me_y, me_c] = line[...]
-    ring = (1, 7, 2, 6, 3, 5, 4)
-    for turn in ring:
+    summed = parts[0] + parts[1] + parts[2] + parts[3]
+    me_core, me_chip = me_vol % VOL_C, me_vol // VOL_C
+    for c in range(CHUNKS):
+        line[c] = summed[:, c * SPAN:(c + 1) * SPAN]
+        lines[c, me_core, me_chip] = line[c]
+    for c in range(CHUNKS):
+
+        def fan(t, carry, c=c):
+            pltpu.make_async_remote_copy(
+                src_ref=line.at[c],
+                dst_ref=lines.at[c, me_core, me_chip],
+                send_sem=row_send.at[c],
+                recv_sem=row_recv.at[c],
+                device_id={"vol": wrap(me_vol + VOL_C * t, VOL)},
+                device_id_type=MESH,
+            ).start()
+            return carry
+
+        lax.fori_loop(1, VOL // VOL_C, fan, 0)
+
+    def hand_over(c):
+        settle(lines.at[c, 0, pl.ds(0, VOL // VOL_C - 1)], row_recv.at[c])
         pltpu.make_async_remote_copy(
-            src_ref=line,
-            dst_ref=lines.at[me_z, me_y, me_c],
-            send_sem=z_send,
-            recv_sem=z_recv.at[turn],
-            device_id={"vol": at_vol(wrap(me_z + turn, VOL_Z), me_y, me_c)},
+            src_ref=lines.at[c, me_core],
+            dst_ref=lines.at[c, me_core],
+            send_sem=core_send.at[c],
+            recv_sem=core_recv.at[c],
+            device_id={"vol": me_chip * VOL_C + 1 - me_core},
             device_id_type=MESH,
         ).start()
 
-    def to_core(source, target):
-        pltpu.make_async_remote_copy(
-            src_ref=source,
-            dst_ref=target,
-            send_sem=core_send,
-            recv_sem=core_recv,
-            device_id={"vol": at_vol(me_z, me_y, 1 - me_c)},
-            device_id_type=MESH,
-        ).start()
-
-    for turn in (0,) + ring:
-        z = wrap(me_z + VOL_Z - turn, VOL_Z)
-        target = lines.at[z, me_y, me_c]
-        source = line if turn == 0 else target
-        if turn:
-            settle(target, z_recv.at[turn])
-        for step in (2, 1, 3):
-            pltpu.make_async_remote_copy(
-                src_ref=source,
-                dst_ref=target,
-                send_sem=y_send,
-                recv_sem=y_recv.at[step],
-                device_id={"vol": at_vol(me_z, wrap(me_y + step, VOL_Y), me_c)},
-                device_id_type=MESH,
-            ).start()
-        to_core(source, target)
-    for step in (1, 3, 2):
-        y = wrap(me_y + VOL_Y - step, VOL_Y)
-        column = lines.at[:, y, me_c]
-        settle(column, y_recv.at[step])
-        to_core(column, column)
-    settle(lines.at[:, :, 0], core_recv)
-    settle(lines.at[pl.ds(0, VOL_Z - 1), 0, 0], z_send)
-    settle(lines.at[:, pl.ds(0, VOL_Y - 1), 0], y_send)
-    settle(lines.at[:, :, 0], core_send)
+    span = []
+
+    def edges_of(c):
+        settle(lines.at[c, 0], core_recv.at[c])
+        whole = dot3(mm, sine_rows[...], lines[c].reshape(VOL, SPAN))
+        tiles_here = [whole[:, t * LANES:(t + 1) * LANES] for t in range(TILES)]
+        span.extend(tiles_here)
+        across = dot3(mm, first[...], whole)
+        across = jnp.concatenate(
+            [across[:, t * LANES:(t + 1) * LANES] * lane_power[...] for t in range(TILES)], 0
+        ).reshape(TILES, 8, LANES)
+        along = jnp.concatenate(
+            [dot3(mm_nt, pair_first[...], tile) * pair_power[...] for tile in tiles_here], 0
+        ).reshape(TILES, 16, CTRL)
+        row_sum = [None, None]
+        col_sum = [[None, None], [None, None]]
+        for n in range(3):
+            for side in range(2):
+                term = across[:, 2 * n + side, :]
+                row_sum[side] = term if n == 0 else row_sum[side] + term
+                at = n * 4 * CTRL + side * CTRL
+                edges[c, 0:TILES, at:at + CTRL] = row_sum[side][:, 0:CTRL]
+                edges[c, TILES:PIECE, at:at + CTRL] = row_sum[side][:, CTRL:]
+                for half in range(2):
+                    term = along[:, 6 * half + 2 * n + side, :]
+                    col_sum[half][side] = term if n == 0 else col_sum[half][side] + term
+                    at = n * 4 * CTRL + (2 + side) * CTRL
+                    edges[c, half * TILES:(half + 1) * TILES, at:at + CTRL] = col_sum[half][side]
+        all_edges[c, pl.ds(me_dsg, 1)] = edges[c][None]
+        dsg_start(1 + c, lambda peer: edges.at[c], all_edges.at[c])
 
     for load in loads[1:]:
         load.wait()
-    whole = dot3(mm, sine[...], lines[...].reshape(VOL, ROW))
-    span = [whole[:, t * LANES:(t + 1) * LANES] for t in range(HALF)]
-    across = dot3(mm, first[...], whole)
-    row_parts = [[], [], []]
-    col_parts = [[], [], []]
-    stacked = jnp.concatenate([across[:, t * LANES:(t + 1) * LANES] * lane_power[...] for t in range(HALF)], 0)
-    edges_rows = stacked.reshape(HALF, 8, LANES)
-    along = jnp.concatenate([dot3(mm_nt, pair_first[...], span[t]) * pair_power[...] for t in range(HALF)], 0)
-    edges_cols = along.reshape(HALF, 16, CTRL)
-    row_sum = [None, None]
-    col_sum = [[None, None], [None, None]]
-    for n in range(3):
-        for side in range(2):
-            term = edges_rows[:, 2 * n + side, :]
-            row_sum[side] = term if n == 0 else row_sum[side] + term
-            at = n * 4 * CTRL + side * CTRL
-            edges[0:HALF, at:at + CTRL] = row_sum[side][:, 0:CTRL]
-            edges[HALF:OWN, at:at + CTRL] = row_sum[side][:, CTRL:]
-            for half in range(2):
-                term = edges_cols[:, 6 * half + 2 * n + side, :]
-                col_sum[half][side] = term if n == 0 else col_sum[half][side] + term
-                at = n * 4 * CTRL + (2 + side) * CTRL
-                edges[half * HALF:(half + 1) * HALF, at:at + CTRL] = col_sum[half][side]
-    all_edges[pl.ds(me_dsg, 1)] = edges[...][None]
-    dsg_start(1, lambda peer: edges, all_edges)
+    hand_over(0)
+    hand_over(1)
+    edges_of(0)
+    hand_over(2)
+    edges_of(1)
+    edges_of(2)
+    for c in range(CHUNKS):
+        settle(lines.at[c, 0, pl.ds(0, VOL // VOL_C - 1)], row_send.at[c])
+        settle(lines.at[c, 0], core_send.at[c])
+
     calm = dot3(mm, jnp.concatenate([tile * total_pair[...] for tile in span], 0), sine_pair[...])
     for t in range(HALF):
         design_out[t] = dot3(mm, sine[...], calm[t * CTRL:(t + 1) * CTRL])
     first_free = dot3(mm, first[...], sine[...])
     pair_first_free = dot3(mm, pair_first[...], sine_pair[...])
-    dsg_wait(1, all_edges)
-
-    base = all_edges[...].reshape(PATCHES, 12 * CTRL)
+    for c in range(CHUNKS):
+        dsg_wait(1 + c, all_edges.at[c])
+
+    base = jnp.concatenate([all_edges[c, owner] for owner in range(DSG) for c in range(CHUNKS)], 0)
 
     def exchange(edge):
         taken = []
@@ -497,14 +508,17 @@
         own = halo[2 - k, mine, :]
         for side in range(2):
             row = 2 * k + side
-            at = side * CTRL
-            pair = jnp.concatenate([own[0:HALF, at:at + CTRL], own[HALF:OWN, at:at + CTRL]], 1)
-            halo_rows[:, row, :] = pair * (SMOOTHING * lane_power[row:row + 1, :])
-            at = (2 + side) * CTRL
-            for half in range(2):
-                halo_cols[:, 6 * half + row, :] = own[half * HALF:(half + 1) * HALF, at:at + CTRL] * (
-                    SMOOTHING * pair_power[row:row + 1, :]
-                )
+            for c in range(CHUNKS):
+                here = slice(c * TILES, (c + 1) * TILES)
+                halves = [own[c * PIECE + half * TILES:c * PIECE + (half + 1) * TILES] for half in range(2)]
+                at = side * CTRL
+                pair = jnp.concatenate([half[:, at:at + CTRL] for half in halves], 1)
+                halo_rows[here, row, :] = pair * (SMOOTHING * lane_power[row:row + 1, :])
+                at = (2 + side) * CTRL
+                for half in range(2):
+                    halo_cols[here, 6 * half + row, :] = halves[half][:, at:at + CTRL] * (
+                        SMOOTHING * pair_power[row:row + 1, :]
+                    )
     rows_free = dot3(mm, halo_rows[...].reshape(HALF * 8, LANES), sine_pair[...])
     cols_free = dot3(mm, halo_cols[...].reshape(HALF * 16, CTRL), sine[...])
     for t in range(HALF):
@@ -515,8 +529,12 @@
 
 def finish(far_ref, pair_ref, far_out, design_out):
     far_out[...] = far_ref[...]
-    design_out[0:HALF] = pair_ref[:, :, 0:CTRL]
-    design_out[HALF:OWN] = pair_ref[:, :, CTRL:]
+    for c in range(CHUNKS):
+        for half in range(2):
+            at = c * PIECE + half * TILES
+            design_out[at:at + TILES] = pair_ref[
+                c * TILES:(c + 1) * TILES, :, half * CTRL:(half + 1) * CTRL
+            ]
 
 
 def per_device(
@@ -541,7 +559,7 @@
         scratch_shapes=[pltpu.VMEM(fields.shape, F32)]
         + [pltpu.VMEM(t.shape, F32) for t in tables]
         + [
-            pltpu.VMEM((LANES, LANES), F32),
+            pltpu.VMEM((4, LANES, LANES), F32),
             pltpu.VMEM((CTRL, points), F32),
             pltpu.VMEM((GROUP * CTRL, points), F32),
             pltpu.VMEM((16, LANES), I32),
@@ -555,15 +573,15 @@
             pltpu.VMEM((VOL, 1, GROUP * CTRL), F32),
             pltpu.VMEM((DSG, 1, ROW), F32),
             pltpu.VMEM((DSG, 1, ROW), F32),
-            pltpu.VMEM((1, ROW), F32),
-            pltpu.VMEM((VOL_Z, VOL_Y, VOL_C, 1, ROW), F32),
-            pltpu.VMEM((OWN, 12 * CTRL), F32),
-            pltpu.VMEM((DSG, OWN, 12 * CTRL), F32),
+            pltpu.VMEM((CHUNKS, 1, SPAN), F32),
+            pltpu.VMEM((CHUNKS, VOL_C, VOL // VOL_C, 1, SPAN), F32),
+            pltpu.VMEM((CHUNKS, PIECE, 12 * CTRL), F32),
+            pltpu.VMEM((CHUNKS, DSG, PIECE, 12 * CTRL), F32),
             pltpu.VMEM((3, PATCHES, 4 * CTRL), F32),
             pltpu.VMEM((HALF, 8, LANES), F32),
             pltpu.VMEM((HALF, 16, CTRL), F32),
-            dma((3,)), dma((3,)), dma((2,)), dma((2,)),
-            dma, dma((VOL_Z,)), dma, dma((VOL_Y,)), dma, dma,
+            dma((3,)), dma((3,)), dma((1 + CHUNKS,)), dma((1 + CHUNKS,)),
+            dma((CHUNKS,)), dma((CHUNKS,)), dma((CHUNKS,)), dma((CHUNKS,)),
             dma, dma((len(tables),)), dma,
         ],
         compiler_params=pltpu.CompilerParams(

time: 65.9 us -> 61.5 us (0.933)
  Pallas kernels: 65.1 us -> 60.7 us
    pallas_call x1, Pallas kernels: 63 us -> 58.6 us  [per_device(): pl.pallas_call(kernel, out_shape=(jax.ShapeDtypeStruct((1, far_count), F3...]
where the time goes in v3:
time: 61.5 us; the launch traced here: 61.3 us
  Pallas kernels  60.7 us (99%)
  between operations  0.64 us (1%)
    pallas_call x1, Pallas kernels, per_device(): pl.pallas_call(kernel, out_shape=(jax.ShapeDtypeStruct((1, far_count), F3...  58.6 us
    pallas_call x1, Pallas kernels, per_device(): pl.pallas_call(finish, out_shape=(jax.ShapeDtypeStruct((1, far_count), F3...  2.05 us

profile of v3, /device:TPU:1, one launch (start us, length us, event | category | flops | bytes accessed | tf_op | source)
XLA Modules:
  0.0 61.3 jit_solution(8948452897246029702)
XLA Ops:
  0.6 58.6 %shard_map.194 = (f32[1,512]{1,0:T(1,128)}, f32[12,64,128]{2,1,0:T(8,128)}) custom-call(f32[8,512]{1,0:T(8,128)} %far_geom.1, s32[1,512]{1,0:T(1,128)} %bitcast.9, s32[1,512]{1,0:T(1,128)} %bitcast.10, s32[1,512]{1,0:T(1,128)} %bitcast.11, f32[8,2048]{1,0:T(8,128)} %near_geom.1, s32[16,128]{1,0:T(8,128)} %bitcast.7, s32[1,2048]{1,0:T(1,128)} %bitcast.8, ...), custom_call_target="tpu_custom_call" | custom-call | tf_op jit(solution)/shard_map/pallas_call | solution.py:551
  59.3 2.0 %shard_map.195 = (f32[1,512]{1,0:T(1,128)}, f32[24,64,64]{2,1,0:T(8,128)}) custom-call(f32[1,512]{1,0:T(1,128)} %get-tuple-element.6.far_ref, f32[12,64,128]{2,1,0:T(8,128)} %get-tuple-element.7.pair_ref), custom_call_target="tpu_custom_call" | custom-call | tf_op jit(solution)/shard_map/pallas_call | solution.py:602

commit v4 on v3

--- a/solution.py
+++ b/solution.py
@@ -70,8 +70,9 @@
             for half in range(2):
                 pair_first[6 * half + row, half * CTRL:(half + 1) * CTRL] = power[k] * ends[side]
                 pair_power[6 * half + row] = power[k]
-    by_core = np.concatenate([np.arange(core, VOL, VOL_C) for core in range(VOL_C)])
-    tables = (sine, sine[:, by_core], sine_pair, total_pair, spread(0), spread(1), first, lane_power, pair_first, pair_power)
+    held = np.arange(VOL)
+    held = held % VOL_C * (VOL // VOL_C) + held // VOL_C
+    tables = (sine, sine[held], sine_pair, total_pair, spread(0), spread(1), first, lane_power, pair_first, pair_power)
     return [np.asarray(t, np.float32) for t in tables]
 
 
@@ -107,6 +108,11 @@
     high, middle, low = split3(x)
     picks = picks.astype(BF16)
     return product(picks, high) + product(picks, middle) + product(picks, low)
+
+
+def picked(product, picks, x):
+    high, low = split2(x)
+    return product(picks, high) + product(picks, low)
 
 
 def dot3(product, a, b):
@@ -175,10 +181,10 @@
 
 def kernel(
     far_geom, block, far_cell, far_patch, near_geom, near_cell, near_patch, adjacency,
-    fields_in, sine_in, sine_rows_in, sine_pair_in, total_pair_in, spread0_in, spread1_in, first_in, lane_power_in,
+    fields_in, sine_in, sine_held_in, sine_pair_in, total_pair_in, spread0_in, spread1_in, first_in, lane_power_in,
     pair_first_in, pair_power_in,
     far_out, design_out,
-    fields, sine, sine_rows, sine_pair, total_pair, spread0, spread1, first, lane_power, pair_first, pair_power,
+    fields, sine, sine_held, sine_pair, total_pair, spread0, spread1, first, lane_power, pair_first, pair_power,
     rows, left, right, cells_v, cells_s, dens, ask, asked, reply, replied, grid, grids, part, parts,
     line, lines, edges, all_edges, halo, halo_rows, halo_cols,
     vol_send, vol_recv, dsg_send, dsg_recv, row_send, row_recv, core_send, core_recv,
@@ -195,7 +201,7 @@
         pltpu.make_async_copy(source, target, load_sem.at[i])
         for i, (source, target) in enumerate(
             (
-                (sine_in, sine), (sine_rows_in, sine_rows), (sine_pair_in, sine_pair), (total_pair_in, total_pair),
+                (sine_in, sine), (sine_held_in, sine_held), (sine_pair_in, sine_pair), (total_pair_in, total_pair),
                 (spread0_in, spread0), (spread1_in, spread1), (first_in, first),
                 (lane_power_in, lane_power), (pair_first_in, pair_first), (pair_power_in, pair_power),
             )
@@ -305,8 +311,8 @@
         return rows[slot].T
 
     def scatter(at, strength, s_param, t_param, patch):
-        left[:, pl.ds(at, LANES)] = spline(s_param)
-        weights = spline(t_param)
+        left[:, pl.ds(at, LANES)] = dot3(mm, sine_held[...], spline(s_param))
+        weights = dot3(mm, sine[...], spline(t_param))
         if strength is not None:
             weights = weights * strength
         for s in range(GROUP):
@@ -323,12 +329,14 @@
         return carry
 
     load_fields.wait()
+    for load in loads:
+        load.wait()
     chunks = near_count // LANES
-    lax.fori_loop(0, chunks // 4, near_chunk, 0)
+    lax.fori_loop(0, 11, near_chunk, 0)
 
     pl.semaphore_wait(barrier, VOL - 1 + DSG - 1)
     vol_start(0, ask, asked)
-    lax.fori_loop(chunks // 4, 5 * chunks // 8, near_chunk, 0)
+    lax.fori_loop(11, 14, near_chunk, 0)
 
     vol_wait(0, ask, asked)
     wanted = asked[:, 0, :].T
@@ -356,7 +364,7 @@
     replied[pl.ds(me_vol, 1)] = reply[pl.ds(me_vol, 1)]
     vol_start(1, reply, replied)
 
-    lax.fori_loop(5 * chunks // 8, chunks, near_chunk, 0)
+    lax.fori_loop(14, chunks, near_chunk, 0)
     near_grid = dot3(mm_nt, left[:, 0:near_count], right[:, 0:near_count])
 
     for t in range(far_count // LANES):
@@ -390,10 +398,8 @@
     got = grids[:, 0, :]
     total = None
     for s in range(GROUP):
-        term = exact(mm, places[s], got[:, s * CTRL:(s + 1) * CTRL])
+        term = picked(mm, places[s], got[:, s * CTRL:(s + 1) * CTRL])
         total = term if total is None else total + term
-    loads[0].wait()
-    total = dot3(mm, total, sine[...])
     for owner in range(DSG):
         base = owner * OWN
         for t in range(HALF):
@@ -438,7 +444,7 @@
 
     def edges_of(c):
         settle(lines.at[c, 0], core_recv.at[c])
-        whole = dot3(mm, sine_rows[...], lines[c].reshape(VOL, SPAN))
+        whole = lines[c].reshape(VOL, SPAN)
         tiles_here = [whole[:, t * LANES:(t + 1) * LANES] for t in range(TILES)]
         span.extend(tiles_here)
         across = dot3(mm, first[...], whole)
@@ -465,8 +471,6 @@
         all_edges[c, pl.ds(me_dsg, 1)] = edges[c][None]
         dsg_start(1 + c, lambda peer: edges.at[c], all_edges.at[c])
 
-    for load in loads[1:]:
-        load.wait()
     hand_over(0)
     hand_over(1)
     edges_of(0)
@@ -477,6 +481,8 @@
         settle(lines.at[c, 0, pl.ds(0, VOL // VOL_C - 1)], row_send.at[c])
         settle(lines.at[c, 0], core_send.at[c])
 
+    halo_rows[...] = jnp.zeros((HALF, 8, LANES), F32)
+    halo_cols[...] = jnp.zeros((HALF, 16, CTRL), F32)
     calm = dot3(mm, jnp.concatenate([tile * total_pair[...] for tile in span], 0), sine_pair[...])
     for t in range(HALF):
         design_out[t] = dot3(mm, sine[...], calm[t * CTRL:(t + 1) * CTRL])
@@ -491,7 +497,7 @@
         taken = []
         for side in range(4):
             other = side ^ 1
-            taken.append(exact(mm, facing[side], edge[:, other * CTRL:(other + 1) * CTRL]))
+            taken.append(picked(mm, facing[side], edge[:, other * CTRL:(other + 1) * CTRL]))
         return jnp.concatenate(taken, 1)
 
     width = 4 * CTRL
@@ -501,8 +507,6 @@
         base[:, 2 * width:] + dot3(mm, halo0, spread1[...]) + dot3(mm, halo1, spread0[...])
     )
     halo[0], halo[1], halo[2] = halo0, halo1, halo2
-    halo_rows[...] = jnp.zeros((HALF, 8, LANES), F32)
-    halo_cols[...] = jnp.zeros((HALF, 16, CTRL), F32)
     mine = pl.ds(pl.multiple_of(me_dsg * OWN, 8), OWN)
     for k in range(3):
         own = halo[2 - k, mine, :]

time: 61.5 us -> 59.6 us (0.969)
  Pallas kernels: 60.7 us -> 58.8 us
    pallas_call x1, Pallas kernels: 58.6 us -> 56.8 us  [per_device(): pl.pallas_call(kernel, out_shape=(jax.ShapeDtypeStruct((1, far_count), F3...]
where the time goes in v4:
time: 59.6 us; the launch traced here: 59.4 us
  Pallas kernels  58.8 us (99%)
  between operations  0.64 us (1%)
    pallas_call x1, Pallas kernels, per_device(): pl.pallas_call(kernel, out_shape=(jax.ShapeDtypeStruct((1, far_count), F3...  56.8 us
    pallas_call x1, Pallas kernels, per_device(): pl.pallas_call(finish, out_shape=(jax.ShapeDtypeStruct((1, far_count), F3...  2.05 us

profile of v4, /device:TPU:1, one launch (start us, length us, event | category | flops | bytes accessed | tf_op | source)
XLA Modules:
  0.0 59.4 jit_solution(2183049248388390266)
XLA Ops:
  0.6 56.8 %shard_map.194 = (f32[1,512]{1,0:T(1,128)}, f32[12,64,128]{2,1,0:T(8,128)}) custom-call(f32[8,512]{1,0:T(8,128)} %far_geom.1, s32[1,512]{1,0:T(1,128)} %bitcast.9, s32[1,512]{1,0:T(1,128)} %bitcast.10, s32[1,512]{1,0:T(1,128)} %bitcast.11, f32[8,2048]{1,0:T(8,128)} %near_geom.1, s32[16,128]{1,0:T(8,128)} %bitcast.7, s32[1,2048]{1,0:T(1,128)} %bitcast.8, ...), custom_call_target="tpu_custom_call" | custom-call | tf_op jit(solution)/shard_map/pallas_call | solution.py:555
  57.4 2.0 %shard_map.195 = (f32[1,512]{1,0:T(1,128)}, f32[24,64,64]{2,1,0:T(8,128)}) custom-call(f32[1,512]{1,0:T(1,128)} %get-tuple-element.6.far_ref, f32[12,64,128]{2,1,0:T(8,128)} %get-tuple-element.7.pair_ref), custom_call_target="tpu_custom_call" | custom-call | tf_op jit(solution)/shard_map/pallas_call | solution.py:606

commit v5 on v4

--- a/solution.py
+++ b/solution.py
@@ -304,10 +304,9 @@
     facing = [jnp.where(patch_lane == sides[:, side:side + 1], 1.0, 0.0).astype(BF16) for side in range(4)]
 
 
-    def take(cells, t, slot, bounded=False):
+    def take(cells, t, slot):
         for r in range(LANES):
-            cell = jnp.clip(cells[t, r], 0, fields.shape[0] - 1) if bounded else cells[t, r]
-            rows[slot, r:r + 1, :] = fields[pl.ds(cell, 1), :]
+            rows[slot, r:r + 1, :] = fields[pl.ds(cells[t, r], 1), :]
         return rows[slot].T
 
     def scatter(at, strength, s_param, t_param, patch):
@@ -353,7 +352,7 @@
     to_scalar.wait()
     dens[...] = jnp.zeros((LANES, LANES), F32)
     for t in range(CAP // 2):
-        columns = take(cells_s, t, t % 4, True)
+        columns = take(cells_s, t, t % 4)
         tile = tiles[t]
         strength = densities(
             columns, [tile[i:i + 1] for i in range(1, 4)], [tile[i:i + 1] for i in range(4, 7)]
@@ -402,10 +401,12 @@
         total = term if total is None else total + term
     for owner in range(DSG):
         base = owner * OWN
-        for t in range(HALF):
-            low = base + t // TILES * PIECE + t % TILES
-            part[owner, :, t * LANES:t * LANES + CTRL] = total[low:low + 1]
-            part[owner, :, t * LANES + CTRL:(t + 1) * LANES] = total[low + TILES:low + TILES + 1]
+        for c in range(CHUNKS):
+            low = base + c * PIECE
+            pair = jnp.concatenate([total[low:low + TILES], total[low + TILES:low + PIECE]], 1)
+            for u in range(TILES):
+                at = (c * TILES + u) * LANES
+                part[owner, :, at:at + LANES] = pair[u:u + 1]
     parts[pl.ds(me_dsg, 1)] = part[pl.ds(me_dsg, 1)]
     dsg_start(0, lambda peer: part.at[peer], parts)
     dsg_wait(0, parts)

time: 59.6 us -> 58.4 us (0.980)
  Pallas kernels: 58.8 us -> 57.6 us
    pallas_call x1, Pallas kernels: 56.8 us -> 55.5 us  [per_device(): pl.pallas_call(kernel, out_shape=(jax.ShapeDtypeStruct((1, far_count), F3...]
where the time goes in v5:
time: 58.4 us; the launch traced here: 58.2 us
  Pallas kernels  57.6 us (99%)
  between operations  0.64 us (1%)
    pallas_call x1, Pallas kernels, per_device(): pl.pallas_call(kernel, out_shape=(jax.ShapeDtypeStruct((1, far_count), F3...  55.5 us
    pallas_call x1, Pallas kernels, per_device(): pl.pallas_call(finish, out_shape=(jax.ShapeDtypeStruct((1, far_count), F3...  2.05 us

profile of v5, /device:TPU:1, one launch (start us, length us, event | category | flops | bytes accessed | tf_op | source)
XLA Modules:
  0.0 58.2 jit_solution(12280409412707645961)
XLA Ops:
  0.6 55.5 %shard_map.194 = (f32[1,512]{1,0:T(1,128)}, f32[12,64,128]{2,1,0:T(8,128)}) custom-call(f32[8,512]{1,0:T(8,128)} %far_geom.1, s32[1,512]{1,0:T(1,128)} %bitcast.9, s32[1,512]{1,0:T(1,128)} %bitcast.10, s32[1,512]{1,0:T(1,128)} %bitcast.11, f32[8,2048]{1,0:T(8,128)} %near_geom.1, s32[16,128]{1,0:T(8,128)} %bitcast.7, s32[1,2048]{1,0:T(1,128)} %bitcast.8, ...), custom_call_target="tpu_custom_call" | custom-call | tf_op jit(solution)/shard_map/pallas_call | solution.py:556
  56.2 2.0 %shard_map.195 = (f32[1,512]{1,0:T(1,128)}, f32[24,64,64]{2,1,0:T(8,128)}) custom-call(f32[1,512]{1,0:T(1,128)} %get-tuple-element.6.far_ref, f32[12,64,128]{2,1,0:T(8,128)} %get-tuple-element.7.pair_ref), custom_call_target="tpu_custom_call" | custom-call | tf_op jit(solution)/shard_map/pallas_call | solution.py:607

commit v6 on v5

--- a/solution.py
+++ b/solution.py
@@ -331,11 +331,11 @@
     for load in loads:
         load.wait()
     chunks = near_count // LANES
-    lax.fori_loop(0, 11, near_chunk, 0)
+    lax.fori_loop(0, 12, near_chunk, 0)
 
     pl.semaphore_wait(barrier, VOL - 1 + DSG - 1)
     vol_start(0, ask, asked)
-    lax.fori_loop(11, 14, near_chunk, 0)
+    lax.fori_loop(12, chunks, near_chunk, 0)
 
     vol_wait(0, ask, asked)
     wanted = asked[:, 0, :].T
@@ -363,7 +363,6 @@
     replied[pl.ds(me_vol, 1)] = reply[pl.ds(me_vol, 1)]
     vol_start(1, reply, replied)
 
-    lax.fori_loop(14, chunks, near_chunk, 0)
     near_grid = dot3(mm_nt, left[:, 0:near_count], right[:, 0:near_count])
 
     for t in range(far_count // LANES):

time: 58.4 us -> 58.7 us (level)
  no operation moved by 1% of the time
where the time goes in v6:
time: 58.7 us; the launch traced here: 58.6 us
  Pallas kernels  57.9 us (99%)
  between operations  0.64 us (1%)
    pallas_call x1, Pallas kernels, per_device(): pl.pallas_call(kernel, out_shape=(jax.ShapeDtypeStruct((1, far_count), F3...  55.9 us
    pallas_call x1, Pallas kernels, per_device(): pl.pallas_call(finish, out_shape=(jax.ShapeDtypeStruct((1, far_count), F3...  2.05 us

profile of v6, /device:TPU:1, one launch (start us, length us, event | category | flops | bytes accessed | tf_op | source)
XLA Modules:
  0.0 58.6 jit_solution(18109832278694587736)
XLA Ops:
  0.6 55.9 %shard_map.194 = (f32[1,512]{1,0:T(1,128)}, f32[12,64,128]{2,1,0:T(8,128)}) custom-call(f32[8,512]{1,0:T(8,128)} %far_geom.1, s32[1,512]{1,0:T(1,128)} %bitcast.9, s32[1,512]{1,0:T(1,128)} %bitcast.10, s32[1,512]{1,0:T(1,128)} %bitcast.11, f32[8,2048]{1,0:T(8,128)} %near_geom.1, s32[16,128]{1,0:T(8,128)} %bitcast.7, s32[1,2048]{1,0:T(1,128)} %bitcast.8, ...), custom_call_target="tpu_custom_call" | custom-call | tf_op jit(solution)/shard_map/pallas_call | solution.py:555
  56.5 2.0 %shard_map.195 = (f32[1,512]{1,0:T(1,128)}, f32[24,64,64]{2,1,0:T(8,128)}) custom-call(f32[1,512]{1,0:T(1,128)} %get-tuple-element.6.far_ref, f32[12,64,128]{2,1,0:T(8,128)} %get-tuple-element.7.pair_ref), custom_call_target="tpu_custom_call" | custom-call | tf_op jit(solution)/shard_map/pallas_call | solution.py:606
